TPU v7x, 32 devices: a whole 2x2x4 slice. The times are simulated.
32 devices in a mesh: groups: 2 (over y), seq: 4 (over z), proj: 2 (over x), chan: 2 (over core).
Axes of the slice: x: 2, y: 2, z: 4, core: 2. Of those that a mesh axis runs over, the one named last changes fastest.
Arguments:
- tokens: bfloat16 [8192, 8192], P('seq', ('proj', 'chan')), may hold values from -6 to 6
- w_proj: bfloat16 [8192, 3, 512], P('proj', None, ('groups', 'chan')), parts along dimension 2, may hold values from -0.0625 to 0.0625
- short_taps: float32 [3, 3, 512], P(None, None, ('groups', 'chan')), parts along dimension 2, may hold values from -3 to 3
- long_filter: bfloat16 [8192, 512], P(('seq', 'proj'), ('groups', 'chan')), parts along dimension 1, may hold values from -0.0625 to 0.0625
- filter_bias: float32 [512], P(('groups', 'chan')), parts along dimension 0, may hold values from -1 to 1
Outputs:
- mixed: bfloat16 [8192, 512], P(('seq', 'proj'), ('groups', 'chan')), parts along dimension 1
There are 2 independent parts, one for each index of `groups`. A program takes and returns all parts, laid end to end along the dimension named above; an argument that names none is the same for every part. Nothing has to cross between parts.
All inputs are finite; a program needn't handle non-finite values.
Results may differ from a plain program's by a relative error of at most 0.0075.
Values may be sent and summed in bfloat16 or wider, within the bound.
No kernel may reach another device: no remote copies, remote signals or barrier semaphores. Data moves between devices by JAX's collectives and lax.ppermute only.
A program may use at most 128 MiB of HBM per device.

v0:
```python
import math

import jax
import jax.numpy as jnp
from jax import lax
from jax.sharding import PartitionSpec as P

precise = lax.Precision.HIGH


def shifted(array, axis, by):
    size = lax.axis_size(axis)
    pairs = [(i, i + by) for i in range(size) if 0 <= i + by < size]
    return lax.ppermute(array, axis, pairs)


def twist_angles(outer, inner, total):
    outer_ids = lax.broadcasted_iota(jnp.int32, (outer, inner), 0)
    inner_ids = lax.broadcasted_iota(jnp.int32, (outer, inner), 1)
    return (outer_ids * inner_ids % total).astype(jnp.float32) * (2.0 * math.pi / total)


def dft_tables(points, direction):
    phases = twist_angles(points, points, points)
    return (jnp.cos(phases), direction * jnp.sin(phases))


def complex_einsum(form, left_re, left_im, right_re, right_im):
    real_out = jnp.einsum(form, left_re, right_re, precision=precise) - jnp.einsum(
        form, left_im, right_im, precision=precise
    )
    imag_out = jnp.einsum(form, left_re, right_im, precision=precise) + jnp.einsum(
        form, left_im, right_re, precision=precise
    )
    return (real_out, imag_out)


def rotate(data_re, data_im, turn_angle):
    cosine = jnp.cos(turn_angle)
    sine_part = jnp.sin(turn_angle)
    return (data_re * cosine - data_im * sine_part, data_re * sine_part + data_im * cosine)


def spectral_product(data_re, data_im, width, along):
    first_re = lax.slice_in_dim(data_re, 0, 2 * width, axis=along)
    first_im = lax.slice_in_dim(data_im, 0, 2 * width, axis=along)
    second_re = lax.slice_in_dim(data_re, 2 * width, 4 * width, axis=along)
    second_im = lax.slice_in_dim(data_im, 2 * width, 4 * width, axis=along)
    return (
        first_re * second_re - first_im * second_im,
        first_re * second_im + first_im * second_re,
    )


def combine_halves(time_re, time_im, width, turn_angle, along):
    even_part = lax.slice_in_dim(time_re, 0, width, axis=along)
    odd_re = lax.slice_in_dim(time_re, width, 2 * width, axis=along)
    odd_im = lax.slice_in_dim(time_im, width, 2 * width, axis=along)
    return 0.5 * (even_part + jnp.cos(turn_angle) * odd_re - jnp.sin(turn_angle) * odd_im)


def shards(tokens, w_proj, short_taps, long_filter, filter_bias):
    whole_cols = lax.all_gather(tokens, "chan", axis=1, tiled=True)
    width_in, triple, channels = w_proj.shape
    weights = w_proj.reshape(width_in, triple * channels)
    parts_proj = lax.axis_size("proj")
    rows_own = tokens.shape[0] // parts_proj
    projected = lax.psum_scatter(
        jnp.dot(whole_cols, weights, preferred_element_type=jnp.float32),
        "proj",
        scatter_dimension=0,
        tiled=True,
    )
    tap_count = short_taps.shape[0]
    taps_flat = short_taps.reshape(tap_count, triple * channels)
    tail_rows = projected[rows_own - (tap_count - 1) :]
    earlier = shifted(tail_rows, ("seq", "proj"), 1)
    extended = jnp.concatenate([earlier, projected], axis=0)
    featured = taps_flat[0] * projected
    for lag_step in range(1, tap_count):
        featured = (
            featured
            + taps_flat[lag_step]
            * extended[tap_count - 1 - lag_step : tap_count - 1 - lag_step + rows_own]
        )
    query_part = featured[:, :channels]
    gated_low = (featured[:, channels : 2 * channels] * featured[:, 2 * channels :]).astype(
        jnp.bfloat16
    )
    gated_rows = gated_low.astype(jnp.float32)
    devices = lax.axis_size(("seq", "proj"))
    seq_len = devices * rows_own
    per_device = channels // devices
    gated_low_cols, filter_low_cols = (
        lax.all_to_all(gated_low.T, ("seq", "proj"), split_axis=0, concat_axis=1, tiled=True),
        lax.all_to_all(long_filter.T, ("seq", "proj"), split_axis=0, concat_axis=1, tiled=True),
    )
    gated_cols = gated_low_cols.astype(jnp.float32)
    filter_cols = filter_low_cols.astype(jnp.float32)
    full_angle = lax.broadcasted_iota(jnp.int32, (1, seq_len), 1).astype(jnp.float32) * (
        math.pi / seq_len
    )
    zero_cols = jnp.zeros_like(gated_cols)
    umod_re, umod_im = rotate(gated_cols, zero_cols, -full_angle)
    hmod_re, hmod_im = rotate(filter_cols, zero_cols, -full_angle)
    series_re = jnp.concatenate([gated_cols, umod_re, filter_cols, hmod_re], axis=0)
    series_im = jnp.concatenate([zero_cols, umod_im, zero_cols, hmod_im], axis=0)
    grid_re = series_re.reshape(4 * per_device, devices, rows_own)
    grid_im = series_im.reshape(4 * per_device, devices, rows_own)
    outer_re, outer_im = dft_tables(devices, -1.0)
    inner_re, inner_im = dft_tables(rows_own, -1.0)
    twist = twist_angles(devices, rows_own, seq_len)
    grid_re, grid_im = complex_einsum("kd,cdj->ckj", outer_re, outer_im, grid_re, grid_im)
    grid_re, grid_im = rotate(grid_re, grid_im, -twist)
    grid_re, grid_im = complex_einsum("ckj,jq->ckq", grid_re, grid_im, inner_re, inner_im)
    spec_re, spec_im = spectral_product(grid_re, grid_im, per_device, 0)
    back_inner_re, back_inner_im = dft_tables(rows_own, 1.0)
    back_outer_re, back_outer_im = dft_tables(devices, 1.0)
    back_re, back_im = complex_einsum("ckq,qj->ckj", spec_re, spec_im, back_inner_re, back_inner_im)
    back_re, back_im = rotate(back_re, back_im, twist)
    back_re, back_im = complex_einsum("dk,ckj->cdj", back_outer_re, back_outer_im, back_re, back_im)
    time_re = back_re.reshape(2 * per_device, seq_len) * (1.0 / seq_len)
    time_im = back_im.reshape(2 * per_device, seq_len) * (1.0 / seq_len)
    long_cols = combine_halves(time_re, time_im, per_device, full_angle, 0)
    long_rows = lax.all_to_all(long_cols, ("seq", "proj"), split_axis=1, concat_axis=0, tiled=True)
    long_conv = long_rows.T
    result = query_part * (long_conv + filter_bias * gated_rows)
    return result.astype(jnp.bfloat16)


def solution(mesh):
    placed = (
        P("seq", ("proj", "chan")),
        P("proj", None, ("groups", "chan")),
        P(None, None, ("groups", "chan")),
        P(("seq", "proj"), ("groups", "chan")),
        P(("groups", "chan")),
    )
    return jax.shard_map(
        shards,
        mesh=mesh,
        in_specs=placed,
        out_specs=P(("seq", "proj"), ("groups", "chan")),
        check_vma=False,
    )
```

profile of v0, /device:TPU:0, one launch (start us, length us, event | category | flops | bytes accessed | tf_op | source)
XLA Modules:
  0.0 313.0 jit_solution(15190194606105853624)
XLA Ops:
  6.5 0.7 all-gather.2.cloned.1.call-update
  7.3 1.1 copy-done
  8.4 2.9 copy.14
  11.3 30.4 %all-gather.2.cloned.1.call-done = bf16[2048,4096]{1,0:T(8,128)(2,1)} async-done(((bf16[2048,2048]{1,0:T(8,128)(2,1)}), bf16[2048,4096]{1,0:T(8,128)(2,1)}) %all-gather.2.cloned.1.call-update) | async-done | bytes 16777232 | tf_op jit(solution)/shard_map/all_gather | solution.py:63
  41.7 14.5 %fusion.186 = f32[2048,384]{1,0:T(8,128)} fusion(bf16[2048,4096]{1,0:T(8,128)(2,1)} %all-gather.2.cloned.1.call-done, bf16[4096,384]{0,1:T(8,128)(2,1)} %bitcast.120), kind=kOutput, calls=%fused_computation.202 | convolution fusion | flops 6442450944 | bytes 23068672 | tf_op jit(solution)/shard_map/dot_general | solution.py:69
  56.2 0.9 copy.17
  57.1 5.8 %all-to-all-start.1 = ((bf16[8,16,1024]{2,1,0:T(8,128)(2,1)}), bf16[8,16,1024]{2,1,0:T(8,128)(2,1)S(1)}, u32[]{:S(2)}, u32[]{:S(2)}) async-start(bf16[8,16,1024]{2,1,0:T(8,128)(2,1)} %bitcast.8), calls=%async_computation.2 | async-start | bytes 524288 | tf_op jit(solution)/shard_map/all_to_all | solution.py:96
  63.2 40.5 %reduce-scatter.2.cloned.1.call-done = f32[1024,384]{1,0:T(8,128)} async-done(((f32[2048,384]{1,0:T(8,128)}), f32[1024,384]{1,0:T(8,128)}) %reduce-scatter.2.cloned.1.call-update) | async-done | bytes 1572880 | tf_op jit(solution)/shard_map/reduce_scatter | solution.py:68
  104.4 2.2 collective-permute-start
  106.8 1.1 collective-permute-done
  108.0 3.2 %fusion.45 = f32[1024,384]{1,0:T(8,128)S(1)} fusion(f32[2,384]{1,0:T(2,128)S(1)} %collective-permute-done, f32[1024,384]{1,0:T(8,128)} %reduce-scatter.2.cloned.1.call-done, f32[384]{0:T(512)S(1)} %get-tuple-element.16, f32[384]{0:T(512)S(1)} %get-tuple-element.17, f32[384]{0:T(512)S(1)} %get-tuple-element.15), kind=kLoop, calls=%fused_computation.48 | loop fusion | flops 2752512 | bytes 3153408 | tf_op jit(solution)/shard_map/add | solution.py:82
  111.2 0.8 copy.15
  112.1 7.6 %all-to-all-start = ((bf16[8,16,1024]{2,1,0:T(8,128)(2,1)}), bf16[8,16,1024]{2,1,0:T(8,128)(2,1)S(1)}, u32[]{:S(2)}, u32[]{:S(2)}) async-start(bf16[8,16,1024]{2,1,0:T(8,128)(2,1)} %bitcast.5), calls=%async_computation.1 | async-start | bytes 524288 | tf_op jit(solution)/shard_map/all_to_all | solution.py:95
  120.2 7.6 %all-to-all-done = bf16[8,16,1024]{2,1,0:T(8,128)(2,1)S(1)} async-done(((bf16[8,16,1024]{2,1,0:T(8,128)(2,1)}), bf16[8,16,1024]{2,1,0:T(8,128)(2,1)S(1)}, u32[]{:S(2)}, u32[]{:S(2)}) %all-to-all-start) | async-done | bytes 262176 | tf_op jit(solution)/shard_map/all_to_all | solution.py:95
  128.3 1.2 fusion.63
  129.5 1.2 fusion.64
  130.8 1.3 fusion.41
  132.2 1.3 fusion.40
  133.5 19.3 %fusion.7 = f32[64,8,1024]{2,1,0:T(8,128)S(1)} fusion(f32[64,1024,8]{1,2,0:T(8,128)S(1)} %fusion.41, f32[64,1024,8]{1,2,0:T(8,128)S(1)} %fusion.40, f32[8,1024]{1,0:T(8,128)S(1)} %get-tuple-element.22, f32[8,1024]{1,0:T(8,128)S(1)} %get-tuple-element.23), kind=kOutput, calls=%fused_computation.10 | convolution fusion | flops 3238526976 | bytes 6356992 | tf_op jit(solution)/shard_map/ckj,jq->ckq/dot_general | solution.py:32
  152.9 18.9 %fusion.9 = f32[64,8,1024]{2,1,0:T(8,128)S(1)} fusion(f32[64,1024,8]{1,2,0:T(8,128)S(1)} %fusion.41, f32[64,1024,8]{1,2,0:T(8,128)S(1)} %fusion.40, f32[8,1024]{1,0:T(8,128)S(1)} %get-tuple-element.22, f32[8,1024]{1,0:T(8,128)S(1)} %get-tuple-element.23), kind=kOutput, calls=%fused_computation.12 | convolution fusion | flops 3238526976 | bytes 6356992 | tf_op jit(solution)/shard_map/ckj,jq->ckq/dot_general | solution.py:29
  171.8 19.0 %fusion.50 = f32[64,8,1024]{2,1,0:T(8,128)S(1)} fusion(f32[64,8,1024]{2,1,0:T(8,128)S(1)} %fusion.7, f32[64,1024,8]{1,2,0:T(8,128)S(1)} %fusion.41, f32[64,1024,8]{1,2,0:T(8,128)S(1)} %fusion.40, f32[8,1024]{1,0:T(8,128)S(1)} %get-tuple-element.22, f32[8,1024]{1,0:T(8,128)S(1)} %get-tuple-element.23), kind=kOutput, calls=%fused_computation.52 | convolution fusion | flops 3238002688 | bytes 8454144 | tf_op jit(solution)/shard_map/ckj,jq->ckq/dot_general | solution.py:32
  190.8 18.6 %fusion.47 = f32[64,8,1024]{2,1,0:T(8,128)S(1)} fusion(f32[64,8,1024]{2,1,0:T(8,128)S(1)} %fusion.9, f32[64,1024,8]{1,2,0:T(8,128)S(1)} %fusion.41, f32[64,1024,8]{1,2,0:T(8,128)S(1)} %fusion.40, f32[8,1024]{1,0:T(8,128)S(1)} %get-tuple-element.22, f32[8,1024]{1,0:T(8,128)S(1)} %get-tuple-element.23), kind=kOutput, calls=%fused_computation.51 | convolution fusion | flops 3238002688 | bytes 8454144 | tf_op jit(solution)/shard_map/ckj,jq->ckq/dot_general | solution.py:29
  209.9 18.4 %fusion.3 = f32[32,8,1024]{2,1,0:T(8,128)S(1)} fusion(f32[32,8,1024]{2,1,0:T(8,128)S(1)} %get-tuple-element.6), kind=kOutput, calls=%fused_computation.6 | convolution fusion | flops 1625292800 | bytes 2097152 | tf_op jit(solution)/shard_map/ckq,qj->ckj/dot_general | solution.py:32
  228.4 18.2 %fusion.5 = f32[32,8,1024]{2,1,0:T(8,128)S(1)} fusion(f32[32,8,1024]{2,1,0:T(8,128)S(1)} %get-tuple-element.5), kind=kOutput, calls=%fused_computation.8 | convolution fusion | flops 1625292800 | bytes 2097152 | tf_op jit(solution)/shard_map/ckq,qj->ckj/dot_general | solution.py:29
  246.6 18.4 %fusion.60 = f32[32,8,1024]{2,1,0:T(8,128)S(1)} fusion(f32[32,8,1024]{2,1,0:T(8,128)S(1)} %fusion.3, f32[32,8,1024]{2,1,0:T(8,128)S(1)} %get-tuple-element.5), kind=kOutput, calls=%fused_computation.60 | convolution fusion | flops 1625554944 | bytes 3145728 | tf_op jit(solution)/shard_map/ckq,qj->ckj/dot_general | solution.py:32
  265.0 18.4 %fusion.57 = f32[32,8,1024]{2,1,0:T(8,128)S(1)} fusion(f32[32,8,1024]{2,1,0:T(8,128)S(1)} %fusion.5, f32[32,8,1024]{2,1,0:T(8,128)S(1)} %get-tuple-element.6), kind=kOutput, calls=%fused_computation.59 | convolution fusion | flops 1625554944 | bytes 3145728 | tf_op jit(solution)/shard_map/ckq,qj->ckj/dot_general | solution.py:29
  283.4 0.7 fusion.72
  284.2 0.7 fusion.71
  284.9 0.8 fusion.54
  286.1 0.8 fusion.56
  287.8 16.9 %all_to_all.45 = f32[16,8,1024]{2,0,1:T(8,128)S(1)} all-to-all(f32[16,8,1024]{2,0,1:T(8,128)S(1)} %bitcast.122), channel_id=1, replica_groups=mesh['groups'=2,'seq'=4,'proj'=2,'chan'=2] {'seq','proj'}, dimensions={1} | all-to-all | bytes 1048576 | tf_op jit(solution)/shard_map/all_to_all | solution.py:125
  304.9 0.8 fusion.70
  (32 shorter events, 4.1 us)
Async XLA Ops:
  6.5 1.9 copy-start
  6.5 35.2 %all-gather.2.cloned.1.call-start = ((), (), s32[]{:S(2)}) async-start(), calls=%async_computation.4 | async-start | bytes 25165824 | tf_op jit(solution)/shard_map/all_gather | solution.py:63
  7.3 96.5 %reduce-scatter.2.cloned.1.call-start = ((), (), s32[]{:S(2)}) async-start(), calls=%async_computation.5 | async-start | bytes 4718592 | tf_op jit(solution)/shard_map/reduce_scatter | solution.py:68
  41.7 14.5 %copy-start.1 = (bf16[1024,128]{1,0:T(8,128)(2,1)S(1)}, bf16[1024,128]{1,0:T(8,128)(2,1)}, u32[]{:S(2)}) copy-start(bf16[1024,128]{1,0:T(8,128)(2,1)} %param.8) | copy-start | bytes 786436
  56.2 6.9 %copy-start.2 = (f32[3,3,128]{2,1,0:T(4,128)S(1)}, f32[3,3,128]{2,1,0:T(4,128)}, u32[]{:S(2)}) copy-start(f32[3,3,128]{2,1,0:T(4,128)} %param.7) | copy-start | bytes 13828
  57.1 55.0 %all-to-all-start.1 = ((bf16[8,16,1024]{2,1,0:T(8,128)(2,1)}), bf16[8,16,1024]{2,1,0:T(8,128)(2,1)S(1)}, u32[]{:S(2)}, u32[]{:S(2)}) async-start(bf16[8,16,1024]{2,1,0:T(8,128)(2,1)} %bitcast.8), calls=%async_computation.2 | async-start | bytes 524288 | tf_op jit(solution)/shard_map/all_to_all | solution.py:96
  104.4 3.5 %collective-permute-start = (f32[2,384]{1,0:T(2,128)S(1)}, f32[2,384]{1,0:T(2,128)S(1)}, u32[]{:S(2)}, u32[]{:S(2)}) collective-permute-start(f32[2,384]{1,0:T(2,128)S(1)} %slice.79), channel_id=1, source_target_pairs={{0,2},{2,4},{4,6},{6,8},{8,10},{10,12},{12,14},{1,3},{3,5},{5,7},{... | collective-permute-start | bytes 9224 | tf_op jit(solution)/shard_map/ppermute | solution.py:14
  112.1 15.7 %all-to-all-start = ((bf16[8,16,1024]{2,1,0:T(8,128)(2,1)}), bf16[8,16,1024]{2,1,0:T(8,128)(2,1)S(1)}, u32[]{:S(2)}, u32[]{:S(2)}) async-start(bf16[8,16,1024]{2,1,0:T(8,128)(2,1)} %bitcast.5), calls=%async_computation.1 | async-start | bytes 524288 | tf_op jit(solution)/shard_map/all_to_all | solution.py:95
  287.0 17.9 %copy-start.3 = (f32[128]{0:T(128)S(1)}, f32[128]{0:T(128)}, u32[]{:S(2)}) copy-start(f32[128]{0:T(128)} %param.9) | copy-start | bytes 1540
Sparse Core Ops, SparseCore 0:
  8.9 32.7 all-gather.1
  56.4 47.3 reduce-scatter.1
where the time goes:
time: 317 us; the launch traced here: 313 us
  matrix products  172 us (54%)
  waiting for transfers between devices  80.5 us (25%)
  blocking collectives  16.9 us (5%)
  starting transfers between devices  15.6 us (5%)
  between operations  14.2 us (4%)
  local copies, waits for them, and re-layouts  7.73 us (2%)
  other arithmetic  6.06 us (2%)
    reduce_scatter x1, waiting for transfers between devices, shards(): lax.psum_scatter(jnp.dot(whole_cols, weights, preferred_element_type=jnp....  40.5 us
    dot_general x4, matrix products, complex_einsum(): jnp.einsum(form, left_re, right_im, precision=precise)  39.9 us
    dot_general x4, matrix products, complex_einsum(): jnp.einsum(form, left_im, right_re, precision=precise)  39.5 us
    dot_general x4, matrix products, complex_einsum(): jnp.einsum(form, left_im, right_im, precision=precise)  39.2 us
    dot_general x4, matrix products, complex_einsum(): jnp.einsum(form, left_re, right_re, precision=precise)  39 us
    all_gather x1, waiting for transfers between devices, shards(): whole_cols = lax.all_gather(tokens, 'chan', axis=1, tiled=True)  30.4 us
    all_to_all x1, blocking collectives, shards(): lax.all_to_all(long_cols, ('seq', 'proj'), split_axis=1, concat_axis=0, t...  16.9 us
    dot_general x1, matrix products, shards(): jnp.dot(whole_cols, weights, preferred_element_type=jnp.float32)  14.5 us
  transfers between devices with their start and end apart: 5, of which 4 were waited for; matrix products, arithmetic and copies ran while one was open for 3% of the time, Pallas kernels for 0%

commit v1 on v0

v1 whole, which is shorter than its diff:
```python
import functools

import jax
import jax.numpy as jnp
from jax import lax
from jax.experimental import pallas as pl
from jax.experimental.pallas import tpu as pltpu
from jax.sharding import PartitionSpec as P

LANES = 128
HALO = 16
GROUP = 8
f32 = jnp.float32
bf16 = jnp.bfloat16
RING = ("seq", "proj")


def in_vmem():
    return pl.BlockSpec(memory_space=pltpu.VMEM)


def params(mib):
    return pltpu.CompilerParams(vmem_limit_bytes=mib << 20)


def matmul_body(tok_ref, halo_ref, w_ref, out_ref, *, tile):
    step = pl.program_id(0)
    slabs, _, width = out_ref.shape

    def put(rows, start):
        product = jnp.dot(rows, w_ref[...], preferred_element_type=f32).astype(out_ref.dtype)
        for slab in range(slabs):
            out_ref[slab, pl.ds(start, rows.shape[0]), :] = product[:, slab * width : (slab + 1) * width]

    @pl.when(step == 0)
    def _():
        put(halo_ref[...], 0)

    put(tok_ref[...], pl.multiple_of(HALO + step * tile, HALO))


def matmul(tokens, halo, weights, slabs, dtype):
    rows, depth = tokens.shape
    cols = weights.shape[1]
    tile = min(256, rows)
    out = (slabs, rows + HALO, cols // slabs)
    return pl.pallas_call(
        functools.partial(matmul_body, tile=tile),
        out_shape=jax.ShapeDtypeStruct(out, dtype),
        grid=(rows // tile,),
        in_specs=[
            pl.BlockSpec((tile, depth), lambda i: (i, 0)),
            pl.BlockSpec((HALO, depth), lambda i: (0, 0)),
            pl.BlockSpec((depth, cols), lambda i: (0, 0)),
        ],
        out_specs=pl.BlockSpec(out, lambda i: (0, 0, 0)),
        compiler_params=params(40),
        name="project",
    )(tokens, halo, weights)


def filter_body(h_ref, out_ref, *, order):
    dests, blocks, chans, _ = out_ref.shape
    for block in range(blocks):
        turned = h_ref[block * LANES : (block + 1) * LANES, :].astype(f32).T.astype(bf16)
        for dest in range(dests):
            first = order[dest]
            out_ref[dest, block] = turned[first : first + chans]


def filter_blocks(long_filter, order, chans):
    rows = long_filter.shape[0]
    return pl.pallas_call(
        functools.partial(filter_body, order=order),
        out_shape=jax.ShapeDtypeStruct((len(order), rows // LANES, chans, LANES), bf16),
        in_specs=[in_vmem()],
        out_specs=in_vmem(),
        compiler_params=params(32),
        name="filter_blocks",
    )(long_filter)


def short_conv(padded, taps, start, size):
    total = taps[0:1] * padded[start : start + size, :]
    for lag in range(1, taps.shape[0]):
        total = total + taps[lag : lag + 1] * padded[start - lag : start - lag + size, :]
    return total


def gate_body(kept_ref, got_ref, taps_ref, out_ref, whole):
    dests, blocks, chans, _ = out_ref.shape
    half = dests * chans
    total = kept_ref[...]
    for part in range(got_ref.shape[0]):
        total = total + got_ref[part].astype(f32)
    whole[...] = total
    taps = taps_ref[...]
    for block in range(blocks):
        mixed = short_conv(whole, taps, HALO + block * LANES, LANES).T
        gated = (mixed[:half] * mixed[half:]).astype(bf16)
        for dest in range(dests):
            out_ref[dest, block] = gated[dest * chans : (dest + 1) * chans]


def gate(kept, got, taps, dests):
    rows, width = kept.shape
    blocks = (rows - HALO) // LANES
    return pl.pallas_call(
        gate_body,
        out_shape=jax.ShapeDtypeStruct((dests, blocks, width // 2 // dests, LANES), bf16),
        in_specs=[in_vmem()] * 3,
        out_specs=in_vmem(),
        scratch_shapes=[pltpu.VMEM((rows, width), f32)],
        compiler_params=params(32),
        name="gate",
    )(kept, got, taps)


def conv_body(g_ref, h_ref, bias_ref, out_ref, gs, hs, acc, padded, lhs, toep, *, chans, blocks):
    gs[...] = g_ref[...].astype(f32)
    hs[...] = h_ref[...].astype(f32)
    row = lax.broadcasted_iota(jnp.int32, (LANES, LANES), 0)
    col = lax.broadcasted_iota(jnp.int32, (LANES, LANES), 1)
    keep = col >= row
    padded[0:GROUP, :] = jnp.zeros((GROUP, LANES), f32)
    padded[blocks + GROUP : blocks + 2 * GROUP, :] = jnp.zeros((GROUP, LANES), f32)
    steps = blocks // GROUP

    def channel(c, _):
        series = gs[pl.ds(c, blocks, stride=chans), :]
        padded[GROUP : GROUP + blocks, :] = series
        for r in range(GROUP):
            lhs[:, r * LANES : (r + 1) * LANES] = padded[
                GROUP - r : GROUP - r + blocks + GROUP, :
            ].astype(bf16)
        acc[...] = jnp.zeros_like(acc)

        def build(step, slot, before):
            for r in range(GROUP):
                taps = hs[pl.ds((step * GROUP + r) * chans + c, 1), :]
                turned = pltpu.roll(
                    jnp.broadcast_to(taps, (LANES, LANES)), 0, 1, stride=1, stride_axis=0
                )
                toep[slot, r * LANES : (r + 1) * LANES, :] = jnp.where(keep, turned, before).astype(bf16)
                before = turned
            return before

        before = jnp.zeros((LANES, LANES), f32)
        if steps <= 8:
            for step in range(steps):
                before = build(step, step % 2, before)
                size = min(blocks + GROUP, blocks - step * GROUP)
                acc[step * GROUP : step * GROUP + size, :] += jnp.dot(
                    lhs[0:size, :], toep[step % 2], preferred_element_type=f32
                )
        else:

            def one(step, before):
                before = build(step, 0, before)
                rows = pl.ds(pl.multiple_of(step * GROUP, GROUP), blocks + GROUP)
                acc[rows, :] += jnp.dot(lhs[...], toep[0], preferred_element_type=f32)
                return before

            lax.fori_loop(0, steps, one, before)
        gs[pl.ds(c, blocks, stride=chans), :] = acc[0:blocks, :] + bias_ref[0, c] * series
        return 0

    lax.fori_loop(0, chans, channel, 0)
    out_ref[...] = gs[...].astype(bf16)


def long_conv(gated, filt, bias, chans):
    rows = gated.shape[0]
    blocks = rows // chans
    return pl.pallas_call(
        functools.partial(conv_body, chans=chans, blocks=blocks),
        out_shape=jax.ShapeDtypeStruct((rows, LANES), bf16),
        in_specs=[in_vmem(), in_vmem(), pl.BlockSpec(memory_space=pltpu.SMEM)],
        out_specs=in_vmem(),
        scratch_shapes=[
            pltpu.VMEM((rows, LANES), f32),
            pltpu.VMEM((rows, LANES), f32),
            pltpu.VMEM((2 * blocks + GROUP, LANES), f32),
            pltpu.VMEM((blocks + 2 * GROUP, LANES), f32),
            pltpu.VMEM((blocks + GROUP, GROUP * LANES), bf16),
            pltpu.VMEM((2, GROUP * LANES, LANES), bf16),
        ],
        compiler_params=params(48),
        name="long_conv",
    )(gated, filt, bias)


def finish_body(kept_ref, got_ref, taps_ref, z_ref, out_ref, whole, *, order):
    total = kept_ref[...]
    for part in range(got_ref.shape[0]):
        total = total + got_ref[part].astype(f32)
    whole[...] = total
    taps = taps_ref[...]
    sources = sorted(range(len(order)), key=lambda i: order[i])
    for block in range(z_ref.shape[1]):
        z = jnp.concatenate([z_ref[i, block].astype(f32) for i in sources], axis=0)
        query = short_conv(whole, taps, HALO + block * LANES, LANES)
        out_ref[block * LANES : (block + 1) * LANES, :] = (query * z.T).astype(bf16)


def finish(kept, got, taps, z, order):
    rows, width = kept.shape
    return pl.pallas_call(
        functools.partial(finish_body, order=order),
        out_shape=jax.ShapeDtypeStruct((rows - HALO, width), bf16),
        in_specs=[in_vmem()] * 4,
        out_specs=in_vmem(),
        scratch_shapes=[pltpu.VMEM((rows, width), f32)],
        compiler_params=params(32),
        name="finish",
    )(kept, got, taps, z)


def swap(array, axis, by=1):
    size = lax.axis_size(axis)
    return lax.ppermute(array, axis, [(i, (i + by) % size) for i in range(size)])


def shards(tokens, w_proj, short_taps, long_filter, filter_bias):
    n_proj = lax.axis_size("proj")
    n_seq = lax.axis_size("seq")
    p = lax.axis_index("proj")
    s = lax.axis_index("seq")
    c = lax.axis_index("chan")
    rows, depth = tokens.shape
    own_rows = rows // n_proj
    channels = w_proj.shape[2]
    slab = channels // n_proj
    chans = slab // n_seq
    order = [pp * slab + ss * chans for ss in range(n_seq) for pp in range(n_proj)]

    w = w_proj.transpose(1, 0, 2)

    def by_slab(quarter):
        kv = quarter[1:].reshape(2, depth, n_proj, slab).transpose(1, 2, 0, 3)
        return kv.reshape(depth, 2 * channels), quarter[0]

    own_kv, own_q = by_slab(lax.dynamic_slice_in_dim(w, c * depth, depth, 1))
    out_kv, out_q = by_slab(lax.dynamic_slice_in_dim(w, (1 - c) * depth, depth, 1))
    other_kv, other_q = swap(out_kv, "chan"), swap(out_q, "chan")
    halo = lax.ppermute(tokens[rows - HALO :], "seq", [(i, i + 1) for i in range(n_seq - 1)])

    filt = filter_blocks(long_filter, order, chans)
    filt = lax.all_to_all(filt, RING, split_axis=0, concat_axis=0, tiled=True)

    away = swap(matmul(tokens, halo, other_kv, n_proj, bf16), "chan")
    chip = matmul(tokens, halo, own_kv, n_proj, f32) + away.astype(f32)
    kept = lax.dynamic_index_in_dim(chip, p, 0, keepdims=False)
    got = jnp.stack(
        [
            swap(lax.dynamic_index_in_dim(chip, (p + by) % n_proj, 0, keepdims=False).astype(bf16), "proj", by)
            for by in range(1, n_proj)
        ]
    )

    away_q = swap(matmul(tokens, halo, other_q, 1, bf16), "chan")[0]
    chip_q = matmul(tokens, halo, own_q, 1, f32)[0] + away_q.astype(f32)
    kept_q = lax.dynamic_slice_in_dim(chip_q, p * own_rows, own_rows + HALO, 0)
    got_q = jnp.stack(
        [
            swap(
                lax.dynamic_slice_in_dim(
                    chip_q, ((p + by) % n_proj) * own_rows, own_rows + HALO, 0
                ).astype(bf16),
                "proj",
                by,
            )
            for by in range(1, n_proj)
        ]
    )

    taps_kv = lax.dynamic_slice_in_dim(short_taps[:, 1:], p * slab, slab, 2).reshape(-1, 2 * slab)
    gated = gate(kept, got, taps_kv, n_seq)
    gated = lax.all_to_all(gated, "seq", split_axis=0, concat_axis=0, tiled=True)
    bias = lax.dynamic_slice_in_dim(filter_bias, p * slab + s * chans, chans, 0)[None]
    z = long_conv(gated.reshape(-1, LANES), filt.reshape(-1, LANES), bias, chans)
    z = z.reshape(n_seq * n_proj, -1, chans, LANES)
    z = lax.all_to_all(z, RING, split_axis=0, concat_axis=0, tiled=True)
    return finish(kept_q, got_q, short_taps[:, 0], z, order)


def solution(mesh):
    placed = (
        P("seq", ("proj", "chan")),
        P("proj", None, ("groups", "chan")),
        P(None, None, ("groups", "chan")),
        P(("seq", "proj"), ("groups", "chan")),
        P(("groups", "chan")),
    )
    return jax.shard_map(
        shards,
        mesh=mesh,
        in_specs=placed,
        out_specs=P(("seq", "proj"), ("groups", "chan")),
        check_vma=False,
    )
```

time: 317 us -> 119 us (0.38)
  matrix products: 172 us -> 0 us
  waiting for transfers between devices: 80.5 us -> 23 us
  Pallas kernels: 0 us -> 35.7 us
  local copies, waits for them, and re-layouts: 7.73 us -> 31.7 us
  blocking collectives: 16.9 us -> 0 us
  between operations: 14.2 us -> 0.24 us
  starting transfers between devices: 15.6 us -> 24.9 us
  other arithmetic: 6.06 us -> 2.57 us
    dot_general x17 -> x0, matrix products: 172 us -> none  [the longest x4 39.9 us: complex_einsum(): jnp.einsum(form, left_re, right_im, precision=precise)]
    reduce_scatter x1 -> x0, waiting for transfers between devices: 40.5 us -> none  [shards(): lax.psum_scatter(jnp.dot(whole_cols, weights, preferred_element_type=jnp....]
    pallas_call x0 -> x8, Pallas kernels: none -> 35.7 us  [the longest x1 17.7 us: long_conv(): pl.pallas_call(functools.partial(conv_body, chans=chans, blocks=blocks),...]
    all_gather x1 -> x0, waiting for transfers between devices: 30.4 us -> none  [shards(): whole_cols = lax.all_gather(tokens, 'chan', axis=1, tiled=True)]
    all_to_all x1 -> x0, blocking collectives: 16.9 us -> none  [shards(): lax.all_to_all(long_cols, ('seq', 'proj'), split_axis=1, concat_axis=0, t...]
    ppermute x1 -> x7, waiting for transfers between devices: 1.15 us -> 15.4 us  [the longest x6 13.4 us: swap(): lax.ppermute(array, axis, [(i, (i + by) % size) for i in range(size)])]
    unnamed x13 -> x25, local copies, waits for them, and re-layouts: 5.79 us -> 14.5 us
    ppermute x1 -> x7, starting transfers between devices: 2.22 us -> 9.74 us  [the longest x6 5.25 us: swap(): lax.ppermute(array, axis, [(i, (i + by) % size) for i in range(size)])]
  transfers between devices with their start and end apart: 5 -> 10, of which waited for: 4 -> 4; matrix products, arithmetic and copies ran while one was open for 3% -> 11% of each run, Pallas kernels for 0% -> 11%
where the time goes in v1:
time: 119 us; the launch traced here: 118 us
  Pallas kernels  35.7 us (30%)
  local copies, waits for them, and re-layouts  31.7 us (27%)
  starting transfers between devices  24.9 us (21%)
  waiting for transfers between devices  23 us (19%)
  other arithmetic  2.57 us (2%)
    pallas_call x1, Pallas kernels, long_conv(): pl.pallas_call(functools.partial(conv_body, chans=chans, blocks=blocks),...  17.7 us
    pallas_call x4, Pallas kernels, matmul(): pl.pallas_call(functools.partial(matmul_body, tile=tile), out_shape=jax.S...  15.1 us
    unnamed x25, local copies, waits for them, and re-layouts  14.5 us
    ppermute x6, waiting for transfers between devices, swap(): lax.ppermute(array, axis, [(i, (i + by) % size) for i in range(size)])  13.4 us
    all_to_all x1, waiting for transfers between devices, shards(): lax.all_to_all(gated, 'seq', split_axis=0, concat_axis=0, tiled=True)  7.64 us
    all_to_all x1, starting transfers between devices, shards(): filt = lax.all_to_all(filt, RING, split_axis=0, concat_axis=0, tiled=True)  6.71 us
    ppermute x6, starting transfers between devices, swap(): lax.ppermute(array, axis, [(i, (i + by) % size) for i in range(size)])  5.25 us
    slice x4, local copies, waits for them, and re-layouts, by_slab(): kv = quarter[1:].reshape(2, depth, n_proj, slab).transpose(1, 2, 0, 3)  5.04 us
  transfers between devices with their start and end apart: 10, of which 4 were waited for; matrix products, arithmetic and copies ran while one was open for 11% of the time, Pallas kernels for 11%

profile of v1, /device:TPU:0, one launch (start us, length us, event | category | flops | bytes accessed | tf_op | source)
XLA Modules:
  0.0 118.1 jit_solution(15290407298564650320)
XLA Ops:
  0.0 2.1 %dynamic-slice_bitcast_fusion = (bf16[3,2048,128]{2,1,0:T(8,128)(2,1)S(1)}, bf16[3,2048,128]{2,1,0:T(8,128)(2,1)S(1)}) fusion(bf16[4096,3,128]{2,0,1:T(8,128)(2,1)} %param.6, s32[]{:T(128)S(6)} %select_n.35, s32[]{:T(128)S(6)} %select_n.34), kind=kLoop, calls=%fused_computation.1 | loop fusion | bytes 6291464 | tf_op jit(solution)/shard_map/dynamic_slice | solution.py:244
  2.1 1.1 copy-done.10
  4.3 1.5 %copy.13 = bf16[2,2048,128]{1,2,0:T(8,128)(2,1)S(1)} copy(bf16[2,2048,128]{2,1,0:T(8,128)(2,1)} %slice.31) | data formatting | bytes 2097152 | tf_op jit(solution)/shard_map/slice | solution.py:240
  6.8 1.5 %copy.15 = bf16[2048,256]{1,0:T(8,128)(2,1)S(1)} copy(bf16[2048,256]{0,1:T(8,128)(2,1)} %bitcast.40) | data formatting | bytes 2097152 | tf_op jit(solution)/shard_map/reshape | solution.py:241
  9.6 4.5 %collective-permute-start = (bf16[16,2048]{1,0:T(8,128)(2,1)S(1)}, bf16[16,2048]{1,0:T(8,128)(2,1)S(1)}, u32[]{:S(2)}, u32[]{:S(2)}) collective-permute-start(bf16[16,2048]{1,0:T(8,128)(2,1)S(1)} %slice.21), channel_id=1, source_target_pairs={{0,4},{4,8},{8,12},{1,5},{5,9},{9,13},{2,6},{6,10},{10,14},{3,7},{... | collective-permute-start | bytes 196616 | tf_op jit(solution)/shard_map/ppermute | solution.py:246
  14.1 2.0 %collective-permute-done.halo_ref = bf16[16,2048]{1,0:T(8,128)(2,1)S(1)} collective-permute-done((bf16[16,2048]{1,0:T(8,128)(2,1)S(1)}, bf16[16,2048]{1,0:T(8,128)(2,1)S(1)}, u32[]{:S(2)}, u32[]{:S(2)}) %collective-permute-start) | collective-permute-done | bytes 65568 | tf_op jit(solution)/shard_map/ppermute | solution.py:246
  16.1 3.4 %copy-done.1 = bf16[2048,2048]{1,0:T(8,128)(2,1)S(1)} copy-done((bf16[2048,2048]{1,0:T(8,128)(2,1)S(1)}, bf16[2048,2048]{1,0:T(8,128)(2,1)}, u32[]{:S(2)}) %copy-start.1) | copy-done | bytes 8388632
  19.5 3.9 %project.7 = bf16[2,2064,128]{2,1,0:T(8,128)(2,1)S(1)} custom-call(bf16[2048,2048]{1,0:T(8,128)(2,1)S(1)} %copy-done.1, bf16[16,2048]{1,0:T(8,128)(2,1)S(1)} %collective-permute-done.halo_ref, bf16[2048,256]{1,0:T(8,128)(2,1)S(1)} %collective-permute-done.4.w_ref), custom_call_target="tpu_custom_call" | custom-call | tf_op jit(solution)/shard_map/project/pallas_call | solution.py:47
  23.5 1.9 %slice_bitcast_fusion = bf16[2048,128]{1,0:T(8,128)(2,1)} fusion(bf16[3,2048,128]{2,1,0:T(8,128)(2,1)} %copy-done.10), kind=kLoop, calls=%fused_computation.9 | loop fusion | bytes 1048576 | tf_op jit(solution)/shard_map/squeeze | solution.py:241
  26.7 6.7 %all-to-all-start.1 = ((bf16[8,8,16,128]{3,2,1,0:T(8,128)(2,1)}), bf16[8,8,16,128]{3,2,1,0:T(8,128)(2,1)S(1)}, u32[]{:S(2)}, u32[]{:S(2)}) async-start(bf16[8,8,16,128]{3,2,1,0:T(8,128)(2,1)} %filter_blocks.1), calls=%async_computation.1 | async-start | bytes 524288 | tf_op jit(solution)/shard_map/all_to_all | solution.py:249
  33.4 1.1 slice.30
  34.5 1.5 %copy.10 = bf16[2,2048,128]{1,2,0:T(8,128)(2,1)S(1)} copy(bf16[2,2048,128]{2,1,0:T(8,128)(2,1)} %slice.30) | data formatting | bytes 2097152 | tf_op jit(solution)/shard_map/slice | solution.py:240
  36.0 1.1 copy.11
  37.0 1.5 %copy.12.w_ref = bf16[2048,256]{1,0:T(8,128)(2,1)S(1)} copy(bf16[2048,256]{0,1:T(8,128)(2,1)} %bitcast.42) | data formatting | bytes 2097152 | tf_op jit(solution)/shard_map/reshape | solution.py:241
  38.5 1.1 slice_bitcast_fusion.1.w_ref
  39.6 3.4 %copy-done.2 = bf16[2048,2048]{1,0:T(8,128)(2,1)S(1)} copy-done((bf16[2048,2048]{1,0:T(8,128)(2,1)S(1)}, bf16[2048,2048]{1,0:T(8,128)(2,1)}, u32[]{:S(2)}) %copy-start.2) | copy-done | bytes 8388632
  43.0 3.9 %project.6 = f32[2,2064,128]{2,1,0:T(8,128)S(1)} custom-call(bf16[2048,2048]{1,0:T(8,128)(2,1)S(1)} %copy-done.2, bf16[16,2048]{1,0:T(8,128)(2,1)S(1)} %collective-permute-done.halo_ref, bf16[2048,256]{1,0:T(8,128)(2,1)S(1)} %copy.12.w_ref), custom_call_target="tpu_custom_call" | custom-call | tf_op jit(solution)/shard_map/project/pallas_call | solution.py:47
  48.8 3.6 %project.5 = bf16[1,2064,128]{2,1,0:T(8,128)(2,1)S(1)} custom-call(bf16[2048,2048]{1,0:T(8,128)(2,1)S(1)} %copy-done.2, bf16[16,2048]{1,0:T(8,128)(2,1)S(1)} %collective-permute-done.halo_ref, bf16[2048,128]{1,0:T(8,128)(2,1)S(1)} %copy-done.5), custom_call_target="tpu_custom_call" | custom-call | tf_op jit(solution)/shard_map/project/pallas_call | solution.py:47
  52.5 1.4 %convert_add_fusion = f32[2,2064,128]{2,1,0:T(8,128)S(1)} fusion(f32[2,2064,128]{2,1,0:T(8,128)S(1)} %project.6, bf16[2,2064,128]{2,1,0:T(8,128)(2,1)} %collective-permute-done.5), kind=kLoop, calls=%fused_computation | loop fusion | flops 1056768 | bytes 5283840 | tf_op jit(solution)/shard_map/add | solution.py:252
  53.9 1.3 %copy-done.7 = f32[2,2064,128]{2,1,0:T(8,128)} copy-done((f32[2,2064,128]{2,1,0:T(8,128)}, f32[2,2064,128]{2,1,0:T(8,128)S(1)}, u32[]{:S(2)}) %copy-start.7) | copy-done | bytes 2113560
  56.1 2.0 %collective-permute-start.6 = (bf16[2064,128]{1,0:T(8,128)(2,1)}, bf16[2064,128]{1,0:T(8,128)(2,1)S(1)}, u32[]{:S(2)}, u32[]{:S(2)}) collective-permute-start(bf16[2064,128]{1,0:T(8,128)(2,1)} %fusion), channel_id=1, source_target_pairs={{0,2},{2,0},{1,3},{3,1},{4,6},{6,4},{5,7},{7,5},{8,10},{10,8},{9,1... | collective-permute-start | bytes 1585160 | tf_op jit(solution)/shard_map/ppermute | solution.py:221
  58.4 3.4 %copy-done.3 = bf16[2048,2048]{1,0:T(8,128)(2,1)S(1)} copy-done((bf16[2048,2048]{1,0:T(8,128)(2,1)S(1)}, bf16[2048,2048]{1,0:T(8,128)(2,1)}, u32[]{:S(2)}) %copy-start.3) | copy-done | bytes 8388632
  61.7 3.7 %project.4 = f32[1,2064,128]{2,1,0:T(8,128)S(1)} custom-call(bf16[2048,2048]{1,0:T(8,128)(2,1)S(1)} %copy-done.3, bf16[16,2048]{1,0:T(8,128)(2,1)S(1)} %collective-permute-done.halo_ref, bf16[2048,128]{1,0:T(8,128)(2,1)S(1)} %slice_bitcast_fusion.1.w_ref), custom_call_target="tpu_custom_call" | custom-call | tf_op jit(solution)/shard_map/project/pallas_call | solution.py:47
  65.5 5.5 %collective-permute-done.6 = bf16[2064,128]{1,0:T(8,128)(2,1)S(1)} collective-permute-done((bf16[2064,128]{1,0:T(8,128)(2,1)}, bf16[2064,128]{1,0:T(8,128)(2,1)S(1)}, u32[]{:S(2)}, u32[]{:S(2)}) %collective-permute-start.6) | collective-permute-done | bytes 528416 | tf_op jit(solution)/shard_map/ppermute | solution.py:221
  71.0 1.1 gate.1
  72.1 4.8 %all-to-all-start = ((bf16[4,16,16,128]{3,2,1,0:T(8,128)(2,1)}), bf16[4,16,16,128]{3,2,1,0:T(8,128)(2,1)S(1)}, u32[]{:S(2)}, u32[]{:S(2)}) async-start(bf16[4,16,16,128]{3,2,1,0:T(8,128)(2,1)} %gate.1), calls=%async_computation | async-start | bytes 524288 | tf_op jit(solution)/shard_map/all_to_all | solution.py:279
  76.9 1.1 convert_add_fusion.1
  78.1 7.6 %all-to-all-done = bf16[4,16,16,128]{3,2,1,0:T(8,128)(2,1)S(1)} async-done(((bf16[4,16,16,128]{3,2,1,0:T(8,128)(2,1)}), bf16[4,16,16,128]{3,2,1,0:T(8,128)(2,1)S(1)}, u32[]{:S(2)}, u32[]{:S(2)}) %all-to-all-start) | async-done | bytes 262176 | tf_op jit(solution)/shard_map/all_to_all | solution.py:279
  85.7 17.7 %long_conv.1 = bf16[1024,128]{1,0:T(8,128)(2,1)} custom-call(bf16[1024,128]{1,0:T(8,128)(2,1)S(1)} %bitcast.35, bf16[1024,128]{1,0:T(8,128)(2,1)S(1)} %bitcast.34, f32[1,16]{1,0:T(1,128)S(1)} %dynamic-slice_bitcast_fusion.4.bias_ref), custom_call_target="tpu_custom_call" | custom-call | tf_op jit(solution)/shard_map/long_conv/pallas_call | solution.py:175
  103.5 3.6 %all-to-all-start.2 = ((bf16[8,8,16,128]{3,2,1,0:T(8,128)(2,1)}), bf16[8,8,16,128]{3,2,1,0:T(8,128)(2,1)S(1)}, u32[]{:S(2)}, u32[]{:S(2)}) async-start(bf16[8,8,16,128]{3,2,1,0:T(8,128)(2,1)} %bitcast.20), calls=%async_computation.2 | async-start | bytes 524288 | tf_op jit(solution)/shard_map/all_to_all | solution.py:283
  107.1 2.1 %collective-permute-start.3 = (bf16[1040,128]{1,0:T(8,128)(2,1)S(1)}, bf16[1040,128]{1,0:T(8,128)(2,1)S(1)}, u32[]{:S(2)}, u32[]{:S(2)}) collective-permute-start(bf16[1040,128]{1,0:T(8,128)(2,1)S(1)} %fusion.1), channel_id=1, source_target_pairs={{0,2},{2,0},{1,3},{3,1},{4,6},{6,4},{5,7},{7,5},{8,10},{10,8},{9,1... | collective-permute-start | bytes 798728 | tf_op jit(solution)/shard_map/ppermute | solution.py:221
  109.2 7.9 %collective-permute-done.3 = bf16[1040,128]{1,0:T(8,128)(2,1)S(1)} collective-permute-done((bf16[1040,128]{1,0:T(8,128)(2,1)S(1)}, bf16[1040,128]{1,0:T(8,128)(2,1)S(1)}, u32[]{:S(2)}, u32[]{:S(2)}) %collective-permute-start.3) | collective-permute-done | bytes 266272 | tf_op jit(solution)/shard_map/ppermute | solution.py:221
  (45 shorter events, 9.0 us)
Async XLA Ops:
  0.0 58.3 %copy-start = (f32[128]{0:T(128)S(1)}, f32[128]{0:T(128)}, u32[]{:S(2)}) copy-start(f32[128]{0:T(128)} %param.9) | copy-start | bytes 1540
  2.1 1.2 copy-start.10
  2.1 31.3 %copy-start.9 = (bf16[3,2048,128]{2,1,0:T(8,128)(2,1)}, bf16[3,2048,128]{2,1,0:T(8,128)(2,1)S(1)}, u32[]{:S(2)}) copy-start(bf16[3,2048,128]{2,1,0:T(8,128)(2,1)S(1)} %get-tuple-element.6) | copy-start | bytes 4718596
  8.3 7.8 %collective-permute-start.4 = (bf16[2048,256]{1,0:T(8,128)(2,1)S(1)}, bf16[2048,256]{1,0:T(8,128)(2,1)S(1)}, u32[]{:S(2)}, u32[]{:S(2)}) collective-permute-start(bf16[2048,256]{1,0:T(8,128)(2,1)S(1)} %copy.15), channel_id=1, source_target_pairs={{0,1},{1,0},{2,3},{3,2},{4,5},{5,4},{6,7},{7,6},{8,9},{9,8},{10,11... | collective-permute-start | bytes 3145736 | tf_op jit(solution)/shard_map/ppermute | solution.py:221
  9.6 6.5 %collective-permute-start = (bf16[16,2048]{1,0:T(8,128)(2,1)S(1)}, bf16[16,2048]{1,0:T(8,128)(2,1)S(1)}, u32[]{:S(2)}, u32[]{:S(2)}) collective-permute-start(bf16[16,2048]{1,0:T(8,128)(2,1)S(1)} %slice.21), channel_id=1, source_target_pairs={{0,4},{4,8},{8,12},{1,5},{5,9},{9,13},{2,6},{6,10},{10,14},{3,7},{... | collective-permute-start | bytes 196616 | tf_op jit(solution)/shard_map/ppermute | solution.py:246
  16.1 3.4 %copy-start.1 = (bf16[2048,2048]{1,0:T(8,128)(2,1)S(1)}, bf16[2048,2048]{1,0:T(8,128)(2,1)}, u32[]{:S(2)}) copy-start(bf16[2048,2048]{1,0:T(8,128)(2,1)} %tok_ref.7) | copy-start | bytes 25165828
  19.5 6.3 %copy-start.6 = (bf16[1024,128]{1,0:T(8,128)(2,1)S(1)}, bf16[1024,128]{1,0:T(8,128)(2,1)}, u32[]{:S(2)}) copy-start(bf16[1024,128]{1,0:T(8,128)(2,1)} %h_ref.1) | copy-start | bytes 786436
  23.4 10.0 %copy-start.11 = (f32[3,3,128]{2,1,0:T(4,128)S(1)}, f32[3,3,128]{2,1,0:T(4,128)}, u32[]{:S(2)}) copy-start(f32[3,3,128]{2,1,0:T(4,128)} %param.7) | copy-start | bytes 13828
  23.4 29.1 %collective-permute-start.5 = (bf16[2,2064,128]{2,1,0:T(8,128)(2,1)S(1)}, bf16[2,2064,128]{2,1,0:T(8,128)(2,1)}, u32[]{:S(2)}, u32[]{:S(2)}) collective-permute-start(bf16[2,2064,128]{2,1,0:T(8,128)(2,1)S(1)} %project.7), channel_id=1, source_target_pairs={{0,1},{1,0},{2,3},{3,2},{4,5},{5,4},{6,7},{7,6},{8,9},{9,8},{10,11... | collective-permute-start | bytes 3170312 | tf_op jit(solution)/shard_map/ppermute | solution.py:221
  25.4 21.5 %collective-permute-start.1 = (bf16[2048,128]{1,0:T(8,128)(2,1)}, bf16[2048,128]{1,0:T(8,128)(2,1)S(1)}, u32[]{:S(2)}, u32[]{:S(2)}) collective-permute-start(bf16[2048,128]{1,0:T(8,128)(2,1)} %slice_bitcast_fusion), channel_id=1, source_target_pairs={{0,1},{1,0},{2,3},{3,2},{4,5},{5,4},{6,7},{7,6},{8,9},{9,8},{10,11... | collective-permute-start | bytes 1572872 | tf_op jit(solution)/shard_map/ppermute | solution.py:221
  26.7 45.4 %all-to-all-start.1 = ((bf16[8,8,16,128]{3,2,1,0:T(8,128)(2,1)}), bf16[8,8,16,128]{3,2,1,0:T(8,128)(2,1)S(1)}, u32[]{:S(2)}, u32[]{:S(2)}) async-start(bf16[8,8,16,128]{3,2,1,0:T(8,128)(2,1)} %filter_blocks.1), calls=%async_computation.1 | async-start | bytes 524288 | tf_op jit(solution)/shard_map/all_to_all | solution.py:249
  39.6 3.4 %copy-start.2 = (bf16[2048,2048]{1,0:T(8,128)(2,1)S(1)}, bf16[2048,2048]{1,0:T(8,128)(2,1)}, u32[]{:S(2)}) copy-start(bf16[2048,2048]{1,0:T(8,128)(2,1)} %tok_ref.7) | copy-start | bytes 25165828
  46.9 0.8 copy-start.4
  47.7 1.0 copy-start.5
  52.4 24.5 %collective-permute-start.2 = (bf16[1,2064,128]{2,1,0:T(8,128)(2,1)S(1)}, bf16[1,2064,128]{2,1,0:T(8,128)(2,1)}, u32[]{:S(2)}, u32[]{:S(2)}) collective-permute-start(bf16[1,2064,128]{2,1,0:T(8,128)(2,1)S(1)} %project.5), channel_id=1, source_target_pairs={{0,1},{1,0},{2,3},{3,2},{4,5},{5,4},{6,7},{7,6},{8,9},{9,8},{10,11... | collective-permute-start | bytes 1585160 | tf_op jit(solution)/shard_map/ppermute | solution.py:221
  53.9 1.3 %copy-start.7 = (f32[2,2064,128]{2,1,0:T(8,128)}, f32[2,2064,128]{2,1,0:T(8,128)S(1)}, u32[]{:S(2)}) copy-start(f32[2,2064,128]{2,1,0:T(8,128)S(1)} %convert_add_fusion) | copy-start | bytes 6340612
  56.1 14.9 %collective-permute-start.6 = (bf16[2064,128]{1,0:T(8,128)(2,1)}, bf16[2064,128]{1,0:T(8,128)(2,1)S(1)}, u32[]{:S(2)}, u32[]{:S(2)}) collective-permute-start(bf16[2064,128]{1,0:T(8,128)(2,1)} %fusion), channel_id=1, source_target_pairs={{0,2},{2,0},{1,3},{3,1},{4,6},{6,4},{5,7},{7,5},{8,10},{10,8},{9,1... | collective-permute-start | bytes 1585160 | tf_op jit(solution)/shard_map/ppermute | solution.py:221
  58.4 3.4 %copy-start.3 = (bf16[2048,2048]{1,0:T(8,128)(2,1)S(1)}, bf16[2048,2048]{1,0:T(8,128)(2,1)}, u32[]{:S(2)}) copy-start(bf16[2048,2048]{1,0:T(8,128)(2,1)} %tok_ref.7) | copy-start | bytes 25165828
  61.7 3.7 %copy-start.8 = (f32[2,2064,128]{2,1,0:T(8,128)S(1)}, f32[2,2064,128]{2,1,0:T(8,128)}, u32[]{:S(2)}) copy-start(f32[2,2064,128]{2,1,0:T(8,128)} %copy-done.7) | copy-start | bytes 6340612
  72.1 13.6 %all-to-all-start = ((bf16[4,16,16,128]{3,2,1,0:T(8,128)(2,1)}), bf16[4,16,16,128]{3,2,1,0:T(8,128)(2,1)S(1)}, u32[]{:S(2)}, u32[]{:S(2)}) async-start(bf16[4,16,16,128]{3,2,1,0:T(8,128)(2,1)} %gate.1), calls=%async_computation | async-start | bytes 524288 | tf_op jit(solution)/shard_map/all_to_all | solution.py:279
  78.1 31.1 %slice-start = ((f32[3,3,128]{2,1,0:T(4,128)}), f32[3,1,128]{2,1,0:T(1,128)S(1)}, s32[]{:S(2)}) async-start(f32[3,3,128]{2,1,0:T(4,128)} %param.7), calls=%async_computation.3 | async-start | bytes 3072 | tf_op jit(solution)/shard_map/slice | solution.py:284
  103.5 13.7 %all-to-all-start.2 = ((bf16[8,8,16,128]{3,2,1,0:T(8,128)(2,1)}), bf16[8,8,16,128]{3,2,1,0:T(8,128)(2,1)S(1)}, u32[]{:S(2)}, u32[]{:S(2)}) async-start(bf16[8,8,16,128]{3,2,1,0:T(8,128)(2,1)} %bitcast.20), calls=%async_computation.2 | async-start | bytes 524288 | tf_op jit(solution)/shard_map/all_to_all | solution.py:283
  107.1 10.1 %collective-permute-start.3 = (bf16[1040,128]{1,0:T(8,128)(2,1)S(1)}, bf16[1040,128]{1,0:T(8,128)(2,1)S(1)}, u32[]{:S(2)}, u32[]{:S(2)}) collective-permute-start(bf16[1040,128]{1,0:T(8,128)(2,1)S(1)} %fusion.1), channel_id=1, source_target_pairs={{0,2},{2,0},{1,3},{3,1},{4,6},{6,4},{5,7},{7,5},{8,10},{10,8},{9,1... | collective-permute-start | bytes 798728 | tf_op jit(solution)/shard_map/ppermute | solution.py:221

commit v2 on v1

v2 whole, which is shorter than its diff:
```python
import functools
import math

import jax
import jax.numpy as jnp
from jax import lax
from jax.experimental import pallas as pl
from jax.experimental.pallas import tpu as pltpu
from jax.sharding import PartitionSpec as P

LANES = 128
HALO = 16
GROUP = 8
TILE = 256
BRIEF = pl.CostEstimate(flops=1, transcendentals=0, bytes_accessed=1)
f32 = jnp.float32
bf16 = jnp.bfloat16
RING = ("seq", "proj")


def in_vmem():
    return pl.BlockSpec(memory_space=pltpu.VMEM)


def params(mib):
    return pltpu.CompilerParams(vmem_limit_bytes=mib << 20)


def spread(out_ref, product, at, width):
    slabs, _, wide = out_ref.shape
    part = width // slabs
    for slab in range(slabs):
        pieces = [
            product[:, j * width + slab * part : j * width + (slab + 1) * part]
            for j in range(wide // part)
        ]
        whole = pieces[0] if len(pieces) == 1 else jnp.concatenate(pieces, axis=1)
        out_ref[slab, at : at + product.shape[0], :] = whole.astype(out_ref.dtype)


def project_body(place_ref, tok_ref, *refs, halo):
    if halo:
        halo_ref, w_ref, other_ref, kv_own, kv_away, q_own, q_away, own_w, query_w, sems = refs
    else:
        w_ref, other_ref, kv_own, kv_away, q_own, q_away, own_w, query_w, sems = refs
    rows, depth = tok_ref.shape
    width = w_ref.shape[2]
    start = place_ref[1] * depth
    targets = [(0, query_w, 0), (1, own_w, 0), (2, own_w, width)]
    copies = [
        pltpu.make_async_copy(
            w_ref.at[pick, pl.ds(start, depth), :], target.at[:, pl.ds(at, width)], sems.at[pick]
        )
        for pick, target, at in targets
    ]
    for copy in copies:
        copy.start()
    tile = min(TILE, rows)

    def passes(weights, put):
        if halo:
            put(jnp.dot(halo_ref[...], weights, preferred_element_type=f32), 0)
        for at in range(0, rows, tile):
            product = jnp.dot(tok_ref[at : at + tile, :], weights, preferred_element_type=f32)
            put(product, (HALO if halo else 0) + at)

    def put_query(product, at):
        q_own[at : at + product.shape[0], :] = product[:, :width]
        q_away[at : at + product.shape[0], :] = product[:, width:].astype(bf16)

    passes(other_ref[:, : 2 * width], lambda product, at: spread(kv_away, product, at, width))
    query_w[:, width:] = other_ref[:, 2 * width :]
    for copy in copies:
        copy.wait()
    passes(own_w[...], lambda product, at: spread(kv_own, product, at, width))
    passes(query_w[...], put_query)


def project(place, tokens, halo, w, other, slabs):
    rows, depth = tokens.shape
    width = w.shape[2]
    count = rows + (0 if halo is None else HALO)
    keys = (slabs, count, 2 * width // slabs)
    extra = [] if halo is None else [halo]
    return pl.pallas_call(
        functools.partial(project_body, halo=halo is not None),
        out_shape=(
            jax.ShapeDtypeStruct(keys, f32),
            jax.ShapeDtypeStruct(keys, bf16),
            jax.ShapeDtypeStruct((count, width), f32),
            jax.ShapeDtypeStruct((count, width), bf16),
        ),
        in_specs=[pl.BlockSpec(memory_space=pltpu.SMEM)]
        + [in_vmem()] * (1 + len(extra))
        + [pl.BlockSpec(memory_space=pl.ANY), in_vmem()],
        out_specs=(in_vmem(),) * 4,
        scratch_shapes=[
            pltpu.VMEM((depth, 2 * width), bf16),
            pltpu.VMEM((depth, 2 * width), bf16),
            pltpu.SemaphoreType.DMA((3,)),
        ],
        compiler_params=params(14),
        cost_estimate=BRIEF,
        name="project",
    )(place, tokens, *extra, w, other)


def mix_body(place_ref, own_a, came_a, own_b, came_b, kept_ref, send_ref):
    slabs, rows = own_a.shape[:2]
    p = place_ref[0]

    def put(slab, store):
        last = own_b[slab] + came_b[slab].astype(f32)
        store(pl.ds(0, HALO), last[:HALO])
        store(pl.ds(HALO, rows), own_a[slab] + came_a[slab].astype(f32))
        store(pl.ds(HALO + rows, last.shape[0] - HALO), last[HALO:])

    def keep(at, value):
        kept_ref[at, :] = value

    put(p, keep)
    for by in range(1, slabs):

        def send(at, value):
            send_ref[by - 1, at, :] = value.astype(bf16)

        put(lax.rem(p + by, slabs), send)


def mix(place, own_a, came_a, own_b, came_b):
    slabs, rows, width = own_a.shape
    rows += own_b.shape[1]
    return pl.pallas_call(
        mix_body,
        out_shape=(
            jax.ShapeDtypeStruct((rows, width), f32),
            jax.ShapeDtypeStruct((slabs - 1, rows, width), bf16),
        ),
        in_specs=[pl.BlockSpec(memory_space=pltpu.SMEM)] + [in_vmem()] * 4,
        out_specs=(in_vmem(), in_vmem()),
        compiler_params=params(8),
        cost_estimate=BRIEF,
        name="mix",
    )(place, own_a, came_a, own_b, came_b)


def mix_rows_body(place_ref, own_a, came_a, own_b, came_b, kept_ref, send_ref, whole):
    parts = send_ref.shape[0] + 1
    count = kept_ref.shape[0]
    step = count - HALO
    rows = own_a.shape[0]
    p = place_ref[0]
    last = own_b[...] + came_b[...].astype(f32)
    whole[0:HALO, :] = last[:HALO]
    whole[HALO : HALO + rows, :] = own_a[...] + came_a[...].astype(f32)
    whole[HALO + rows :, :] = last[HALO:]

    def part(i):
        return whole[pl.ds(pl.multiple_of(i * step, HALO), count), :]

    kept_ref[...] = part(p)
    for by in range(1, parts):
        send_ref[by - 1] = part(lax.rem(p + by, parts)).astype(bf16)


def mix_rows(place, own_a, came_a, own_b, came_b, parts):
    rows, width = own_a.shape
    rows += own_b.shape[0]
    count = (rows - HALO) // parts + HALO
    return pl.pallas_call(
        mix_rows_body,
        out_shape=(
            jax.ShapeDtypeStruct((count, width), f32),
            jax.ShapeDtypeStruct((parts - 1, count, width), bf16),
        ),
        in_specs=[pl.BlockSpec(memory_space=pltpu.SMEM)] + [in_vmem()] * 4,
        out_specs=(in_vmem(), in_vmem()),
        scratch_shapes=[pltpu.VMEM((rows, width), f32)],
        compiler_params=params(8),
        cost_estimate=BRIEF,
        name="mix_rows",
    )(place, own_a, came_a, own_b, came_b)


def filter_body(h_ref, out_ref, *, order):
    dests, blocks, chans, _ = out_ref.shape
    for block in range(blocks):
        turned = h_ref[block * LANES : (block + 1) * LANES, :].astype(f32).T.astype(bf16)
        for dest in range(dests):
            first = order[dest]
            out_ref[dest, block] = turned[first : first + chans]


def filter_blocks(long_filter, order, chans):
    rows = long_filter.shape[0]
    return pl.pallas_call(
        functools.partial(filter_body, order=order),
        out_shape=jax.ShapeDtypeStruct((len(order), rows // LANES, chans, LANES), bf16),
        in_specs=[in_vmem()],
        out_specs=in_vmem(),
        compiler_params=params(32),
        cost_estimate=BRIEF,
        name="filter_blocks",
    )(long_filter)


def short_conv(padded, taps, start, size):
    total = taps[0:1] * padded[start : start + size, :]
    for lag in range(1, taps.shape[0]):
        total = total + taps[lag : lag + 1] * padded[start - lag : start - lag + size, :]
    return total


def gate_body(kept_ref, got_ref, taps_ref, out_ref, whole):
    dests, blocks, chans, _ = out_ref.shape
    half = dests * chans
    total = kept_ref[...]
    for part in range(got_ref.shape[0]):
        total = total + got_ref[part].astype(f32)
    whole[...] = total
    taps = taps_ref[...]
    for block in range(blocks):
        mixed = short_conv(whole, taps, HALO + block * LANES, LANES).T
        gated = (mixed[:half] * mixed[half:]).astype(bf16)
        for dest in range(dests):
            out_ref[dest, block] = gated[dest * chans : (dest + 1) * chans]


def gate(kept, got, taps, dests):
    rows, width = kept.shape
    blocks = (rows - HALO) // LANES
    return pl.pallas_call(
        gate_body,
        out_shape=jax.ShapeDtypeStruct((dests, blocks, width // 2 // dests, LANES), bf16),
        in_specs=[in_vmem()] * 3,
        out_specs=in_vmem(),
        scratch_shapes=[pltpu.VMEM((rows, width), f32)],
        compiler_params=params(12),
        cost_estimate=BRIEF,
        name="gate",
    )(kept, got, taps)


def conv_body(g_ref, h_ref, bias_ref, out_ref, gs, hs, *scratch, chans, blocks):
    gs[...] = g_ref[...].astype(f32)
    hs[...] = h_ref[...].astype(f32)
    row = lax.broadcasted_iota(jnp.int32, (LANES, LANES), 0)
    col = lax.broadcasted_iota(jnp.int32, (LANES, LANES), 1)
    keep = col >= row
    steps = blocks // GROUP
    sets = [scratch[i : i + 4] for i in range(0, len(scratch), 4)]
    for acc, padded, lhs, toep in sets:
        padded[0:GROUP, :] = jnp.zeros((GROUP, LANES), f32)
        padded[blocks + GROUP : blocks + 2 * GROUP, :] = jnp.zeros((GROUP, LANES), f32)

    def channels(first, _):
        every = [first + i * (chans // len(sets)) for i in range(len(sets))]
        series = []
        for c, (acc, padded, lhs, toep) in zip(every, sets):
            series.append(gs[pl.ds(c, blocks, stride=chans), :])
            padded[GROUP : GROUP + blocks, :] = series[-1]
            for r in range(GROUP):
                lhs[:, r * LANES : (r + 1) * LANES] = padded[
                    GROUP - r : GROUP - r + blocks + GROUP, :
                ].astype(bf16)
            acc[...] = jnp.zeros_like(acc)

        def build(c, step, target, before):
            for r in range(GROUP):
                taps = hs[pl.ds((step * GROUP + r) * chans + c, 1), :].astype(bf16)
                turned = pltpu.roll(
                    jnp.broadcast_to(taps, (LANES, LANES)), 0, 1, stride=1, stride_axis=0
                )
                target[r * LANES : (r + 1) * LANES, :] = jnp.where(keep, turned, before)
                before = turned
            return before

        none = jnp.zeros((LANES, LANES), bf16)
        if steps <= 8:
            before = [none] * len(sets)
            for step in range(steps):
                size = min(blocks + GROUP, blocks - step * GROUP)
                for i, (c, (acc, padded, lhs, toep)) in enumerate(zip(every, sets)):
                    target = toep.at[step % 2]
                    before[i] = build(c, step, target, before[i])
                    acc[step * GROUP : step * GROUP + size, :] += jnp.dot(
                        lhs[0:size, :], target[...], preferred_element_type=f32
                    )
        else:
            for c, (acc, padded, lhs, toep) in zip(every, sets):

                def one(step, before):
                    before = build(c, step, toep.at[0], before)
                    rows = pl.ds(pl.multiple_of(step * GROUP, GROUP), blocks + GROUP)
                    acc[rows, :] += jnp.dot(lhs[...], toep[0], preferred_element_type=f32)
                    return before

                lax.fori_loop(0, steps, one, none)
        for c, own, (acc, padded, lhs, toep) in zip(every, series, sets):
            gs[pl.ds(c, blocks, stride=chans), :] = acc[0:blocks, :] + bias_ref[0, c] * own
        return 0

    lax.fori_loop(0, chans // len(sets), channels, 0)
    out_ref[...] = gs[...].astype(bf16)


def long_conv(gated, filt, bias, chans):
    rows = gated.shape[0]
    blocks = rows // chans
    together = math.gcd(chans, 4)
    one = [
        pltpu.VMEM((2 * blocks + GROUP, LANES), f32),
        pltpu.VMEM((blocks + 2 * GROUP, LANES), f32),
        pltpu.VMEM((blocks + GROUP, GROUP * LANES), bf16),
        pltpu.VMEM((2, GROUP * LANES, LANES), bf16),
    ]
    return pl.pallas_call(
        functools.partial(conv_body, chans=chans, blocks=blocks),
        out_shape=jax.ShapeDtypeStruct((rows, LANES), bf16),
        in_specs=[in_vmem(), in_vmem(), pl.BlockSpec(memory_space=pltpu.SMEM)],
        out_specs=in_vmem(),
        scratch_shapes=[pltpu.VMEM((rows, LANES), f32), pltpu.VMEM((rows, LANES), f32)] + one * together,
        compiler_params=params(24),
        cost_estimate=BRIEF,
        name="long_conv",
    )(gated, filt, bias)


def finish_body(kept_ref, got_ref, taps_ref, z_ref, out_ref, whole, *, order):
    total = kept_ref[...]
    for part in range(got_ref.shape[0]):
        total = total + got_ref[part].astype(f32)
    whole[...] = total
    taps = taps_ref[...]
    sources = sorted(range(len(order)), key=lambda i: order[i])
    for block in range(z_ref.shape[1]):
        z = jnp.concatenate([z_ref[i, block].astype(f32) for i in sources], axis=0)
        query = short_conv(whole, taps, HALO + block * LANES, LANES)
        out_ref[block * LANES : (block + 1) * LANES, :] = (query * z.T).astype(bf16)


def finish(kept, got, taps, z, order):
    rows, width = kept.shape
    return pl.pallas_call(
        functools.partial(finish_body, order=order),
        out_shape=jax.ShapeDtypeStruct((rows - HALO, width), bf16),
        in_specs=[in_vmem()] * 4,
        out_specs=in_vmem(),
        scratch_shapes=[pltpu.VMEM((rows, width), f32)],
        compiler_params=params(32),
        cost_estimate=BRIEF,
        name="finish",
    )(kept, got, taps, z)


def swap(array, axis, by=1):
    size = lax.axis_size(axis)
    return lax.ppermute(array, axis, [(i, (i + by) % size) for i in range(size)])


def shards(tokens, w_proj, short_taps, long_filter, filter_bias):
    n_proj = lax.axis_size("proj")
    n_seq = lax.axis_size("seq")
    p = lax.axis_index("proj")
    s = lax.axis_index("seq")
    c = lax.axis_index("chan")
    rows, depth = tokens.shape
    own_rows = rows // n_proj
    channels = w_proj.shape[2]
    slab = channels // n_proj
    chans = slab // n_seq
    order = [pp * slab + ss * chans for ss in range(n_seq) for pp in range(n_proj)]

    place = jnp.stack([p, c]).astype(jnp.int32)
    barrier = lax.optimization_barrier

    def exchange(send):
        return jnp.stack([swap(send[by - 1], "proj", by) for by in range(1, n_proj)])

    w = w_proj.transpose(1, 0, 2)
    w_hbm = pltpu.with_memory_space_constraint(w, pltpu.HBM)
    theirs = [
        lax.dynamic_slice(w, (pick, (1 - c) * depth, 0), (1, depth, channels))[0]
        for pick in (1, 2, 0)
    ]
    other = swap(jnp.concatenate(theirs, axis=1), "chan")
    halo = lax.ppermute(tokens[rows - HALO :], "seq", [(i, i + 1) for i in range(n_seq - 1)])

    half = rows // 2
    own_a, away_a, own_qa, away_qa = project(place, tokens[:half], None, w_hbm, other, n_proj)
    came_a = swap(away_a, "chan")
    halo, away_qa = barrier((halo, away_qa))
    own_b, away_b, own_qb, away_qb = project(place, tokens[half:], halo, w_hbm, other, n_proj)
    came_b = swap(away_b, "chan")

    kept, send = mix(place, own_a, came_a, own_b, came_b)
    got = exchange(send)

    long_filter, away_qa, away_qb, send = barrier((long_filter, away_qa, away_qb, send))
    filt = filter_blocks(long_filter, order, chans)
    filt = lax.all_to_all(filt, RING, split_axis=0, concat_axis=0, tiled=True)

    kept_q, send_q = mix_rows(place, own_qa, swap(away_qa, "chan"), own_qb, swap(away_qb, "chan"), n_proj)
    got, filt, send_q = barrier((got, filt, send_q))
    got_q = exchange(send_q)

    taps_kv = lax.dynamic_slice_in_dim(short_taps[:, 1:], p * slab, slab, 2).reshape(-1, 2 * slab)
    gated = gate(kept, got, taps_kv, n_seq)
    gated = lax.all_to_all(gated, "seq", split_axis=0, concat_axis=0, tiled=True)
    gated, got_q = barrier((gated, got_q))
    bias = lax.dynamic_slice_in_dim(filter_bias, p * slab + s * chans, chans, 0)[None]
    z = long_conv(gated.reshape(-1, LANES), filt.reshape(-1, LANES), bias, chans)
    z = z.reshape(n_seq * n_proj, -1, chans, LANES)
    z = lax.all_to_all(z, RING, split_axis=0, concat_axis=0, tiled=True)
    return finish(kept_q, got_q, short_taps[:, 0], z, order)


def solution(mesh):
    placed = (
        P("seq", ("proj", "chan")),
        P("proj", None, ("groups", "chan")),
        P(None, None, ("groups", "chan")),
        P(("seq", "proj"), ("groups", "chan")),
        P(("groups", "chan")),
    )
    return jax.shard_map(
        shards,
        mesh=mesh,
        in_specs=placed,
        out_specs=P(("seq", "proj"), ("groups", "chan")),
        check_vma=False,
    )
```

time: 119 us -> 84.7 us (0.71)
  local copies, waits for them, and re-layouts: 31.7 us -> 10.8 us
  Pallas kernels: 35.7 us -> 26.6 us
  starting transfers between devices: 24.9 us -> 21.7 us
    unnamed x25 -> x19, local copies, waits for them, and re-layouts: 14.5 us -> 4.24 us
    all_to_all x1, waiting for transfers between devices: 0.01 us -> 8.21 us  [shards(): z = lax.all_to_all(z, RING, split_axis=0, concat_axis=0, tiled=True)]
    all_to_all x1, waiting for transfers between devices: 7.64 us -> 0.81 us  [shards(): lax.all_to_all(gated, 'seq', split_axis=0, concat_axis=0, tiled=True)]
    pallas_call x1, Pallas kernels: 17.7 us -> 12.4 us  [long_conv(): pl.pallas_call(functools.partial(conv_body, chans=chans, blocks=blocks),...]
    all_to_all x1, waiting for transfers between devices: 0.01 us -> 4.88 us  [shards(): filt = lax.all_to_all(filt, RING, split_axis=0, concat_axis=0, tiled=True)]
    ppermute x6 -> x7, waiting for transfers between devices: 13.4 us -> 9.46 us  [swap(): lax.ppermute(array, axis, [(i, (i + by) % size) for i in range(size)])]
    pallas_call x4, Pallas kernels: 15.1 us -> 11.3 us  [the longest x2 9 us: project(): pl.pallas_call(functools.partial(project_body, halo=halo is not None), ou...]
    reshape x2 -> x0, local copies, waits for them, and re-layouts: 2.95 us -> none  [by_slab(): return (kv.reshape(depth, 2 * channels), quarter[0])]
  transfers between devices with their start and end apart: 10 -> 11, of which waited for: 4 -> 6; matrix products, arithmetic and copies ran while one was open for 11% -> 6% of each run, Pallas kernels for 11% -> 7%
where the time goes in v2:
time: 84.7 us; the launch traced here: 84.1 us
  Pallas kernels  26.6 us (31%)
  waiting for transfers between devices  23.4 us (28%)
  starting transfers between devices  21.7 us (26%)
  local copies, waits for them, and re-layouts  10.8 us (13%)
  other arithmetic  1.48 us (2%)
    pallas_call x1, Pallas kernels, long_conv(): pl.pallas_call(functools.partial(conv_body, chans=chans, blocks=blocks),...  12.4 us
    ppermute x7, waiting for transfers between devices, swap(): lax.ppermute(array, axis, [(i, (i + by) % size) for i in range(size)])  9.46 us
    pallas_call x2, Pallas kernels, project(): pl.pallas_call(functools.partial(project_body, halo=halo is not None), ou...  9 us
    all_to_all x1, waiting for transfers between devices, shards(): z = lax.all_to_all(z, RING, split_axis=0, concat_axis=0, tiled=True)  8.21 us
    all_to_all x1, starting transfers between devices, shards(): z = lax.all_to_all(z, RING, split_axis=0, concat_axis=0, tiled=True)  4.97 us
    all_to_all x1, waiting for transfers between devices, shards(): filt = lax.all_to_all(filt, RING, split_axis=0, concat_axis=0, tiled=True)  4.88 us
    ppermute x7, starting transfers between devices, swap(): lax.ppermute(array, axis, [(i, (i + by) % size) for i in range(size)])  4.54 us
    ppermute x1, starting transfers between devices, shards(): lax.ppermute(tokens[rows - HALO:], 'seq', [(i, i + 1) for i in range(n_se...  4.47 us
  transfers between devices with their start and end apart: 11, of which 6 were waited for; matrix products, arithmetic and copies ran while one was open for 6% of the time, Pallas kernels for 7%

profile of v2, /device:TPU:0, one launch (start us, length us, event | category | flops | bytes accessed | tf_op | source)
XLA Modules:
  0.0 84.1 jit_solution(9723470132062911368)
XLA Ops:
  0.0 1.5 %dynamic-slice_bitcast_fusion.2 = (bf16[2048,128]{1,0:T(8,128)(2,1)S(1)}, bf16[2048,128]{1,0:T(8,128)(2,1)S(1)}, bf16[2048,128]{1,0:T(8,128)(2,1)S(1)}) fusion(bf16[4096,3,128]{2,0,1:T(8,128)(2,1)} %param.6, s32[]{:T(128)S(6)} %select_n.11), kind=kLoop, calls=%fused_computation.3 | loop fusion | bytes 3145732 | tf_op jit(solution)/shard_map/squeeze | solution.py:383
  1.5 1.4 %pad_maximum_fusion = bf16[2048,384]{1,0:T(8,128)(2,1)} fusion(bf16[2048,128]{1,0:T(8,128)(2,1)S(1)} %get-tuple-element.52, bf16[2048,128]{1,0:T(8,128)(2,1)S(1)} %get-tuple-element.53, bf16[2048,128]{1,0:T(8,128)(2,1)S(1)} %get-tuple-element.51), kind=kLoop, calls=%fused_computation | loop fusion | flops 4718592 | bytes 3145728 | tf_op jit(solution)/shard_map/concatenate | solution.py:386
  2.9 0.5 collective-permute-start
  3.3 0.8 %slice.16 = bf16[16,2048]{1,0:T(8,128)(2,1)S(1)} slice(bf16[2048,2048]{1,0:T(8,128)(2,1)} %param.5), slice={[2032:2048], [0:2048]} | slice | bytes 131072 | tf_op jit(solution)/shard_map/slice | solution.py:387
  4.2 4.5 %collective-permute-start.1 = (bf16[16,2048]{1,0:T(8,128)(2,1)S(1)}, bf16[16,2048]{1,0:T(8,128)(2,1)S(1)}, u32[]{:S(2)}, u32[]{:S(2)}) collective-permute-start(bf16[16,2048]{1,0:T(8,128)(2,1)S(1)} %slice.16), channel_id=1, source_target_pairs={{0,4},{4,8},{8,12},{1,5},{5,9},{9,13},{2,6},{6,10},{10,14},{3,7},{... | collective-permute-start | bytes 196616 | tf_op jit(solution)/shard_map/ppermute | solution.py:387
  8.7 4.0 %fusion = (bf16[1024,2048]{1,0:T(8,128)(2,1)S(1)}, bf16[1024,2048]{1,0:T(8,128)(2,1)S(1)}) fusion(bf16[2048,2048]{1,0:T(8,128)(2,1)} %param.5), kind=kLoop, calls=%fused_computation.8 | loop fusion | bytes 16777216 | tf_op jit(solution)/shard_map/slice | solution.py:393
  12.8 4.3 %project.2 = (f32[2,1024,128]{2,1,0:T(8,128)S(1)}, bf16[2,1024,128]{2,1,0:T(8,128)(2,1)S(1)}, f32[1024,128]{1,0:T(8,128)S(1)}, bf16[1024,128]{1,0:T(8,128)(2,1)S(1)}) custom-call(s32[2]{0:T(128)S(1)} %pad_add_fusion.place_ref, bf16[1024,2048]{1,0:T(8,128)(2,1)S(1)} %get-tuple-element.50.tok_ref, bf16[3,4096,128]{2,1,0:T(8,128)(2,1)} %bitcast.27, ...), custom_call_target="tpu_custom_call" | custom-call | flops 1 | bytes 1 | tf_op jit(solution)/shard_map/project/pallas_call | solution.py:85
  17.1 0.8 copy-done.1
  17.9 4.7 %project.3 = (f32[2,1040,128]{2,1,0:T(8,128)S(1)}, bf16[2,1040,128]{2,1,0:T(8,128)(2,1)S(1)}, f32[1040,128]{1,0:T(8,128)S(1)}, bf16[1040,128]{1,0:T(8,128)(2,1)S(1)}) custom-call(s32[2]{0:T(128)S(1)} %pad_add_fusion.place_ref, bf16[1024,2048]{1,0:T(8,128)(2,1)S(1)} %get-tuple-element.49.tok_ref, bf16[16,2048]{1,0:T(8,128)(2,1)S(1)} %collective-permute-done.1.refs_0_, ...), custom_call_target="tpu_custom_call" | custom-call | flops 1 | bytes 1 | tf_op jit(solution)/shard_map/project/pallas_call | solution.py:85
  22.6 0.3 collective-permute-start.3
  23.2 2.2 %collective-permute-done.2.came_a = bf16[2,1024,128]{2,1,0:T(8,128)(2,1)S(1)} collective-permute-done((bf16[2,1024,128]{2,1,0:T(8,128)(2,1)S(1)}, bf16[2,1024,128]{2,1,0:T(8,128)(2,1)S(1)}, u32[]{:S(2)}, u32[]{:S(2)}) %collective-permute-start.2) | collective-permute-done | bytes 524320 | tf_op jit(solution)/shard_map/ppermute | solution.py:358
  25.4 1.6 %mix.1 = (f32[2064,128]{1,0:T(8,128)S(1)}, bf16[1,2064,128]{2,1,0:T(8,128)(2,1)}) custom-call(s32[2]{0:T(128)S(1)} %pad_add_fusion.place_ref, f32[2,1024,128]{2,1,0:T(8,128)S(1)} %get-tuple-element.32.own_a, bf16[2,1024,128]{2,1,0:T(8,128)(2,1)S(1)} %collective-permute-done.2.came_a, f32[2,1040,128]{2,1,0:T(8,128)S(1)} %get-tuple-element.34.own_b, ...), custom_call_target="tpu_custom_call" | custom-call | flops 1 | bytes 1 | tf_op jit(solution)/shard_map/mix/pallas_call | solution.py:133
  27.0 1.5 %collective-permute-start.6 = (bf16[2064,128]{1,0:T(8,128)(2,1)}, bf16[2064,128]{1,0:T(8,128)(2,1)S(1)}, u32[]{:S(2)}, u32[]{:S(2)}) collective-permute-start(bf16[2064,128]{1,0:T(8,128)(2,1)} %bitcast.6), channel_id=1, source_target_pairs={{0,2},{2,0},{1,3},{3,1},{4,6},{6,4},{5,7},{7,5},{8,10},{10,8},{9,1... | collective-permute-start | bytes 1585160 | tf_op jit(solution)/shard_map/ppermute | solution.py:358
  28.5 0.8 %filter_blocks.1 = bf16[8,8,16,128]{3,2,1,0:T(8,128)(2,1)} custom-call(bf16[1024,128]{1,0:T(8,128)(2,1)S(1)} %copy-done.3), custom_call_target="tpu_custom_call" | custom-call | flops 1 | bytes 1 | tf_op jit(solution)/shard_map/filter_blocks/pallas_call | solution.py:196
  29.3 3.9 %all-to-all-start = ((bf16[8,8,16,128]{3,2,1,0:T(8,128)(2,1)}), bf16[8,8,16,128]{3,2,1,0:T(8,128)(2,1)S(1)}, u32[]{:S(2)}, u32[]{:S(2)}) async-start(bf16[8,8,16,128]{3,2,1,0:T(8,128)(2,1)} %filter_blocks.1), calls=%async_computation | async-start | bytes 524288 | tf_op jit(solution)/shard_map/all_to_all | solution.py:401
  33.2 0.5 collective-permute-start.4
  33.9 1.2 %collective-permute-done.4.came_a = bf16[1024,128]{1,0:T(8,128)(2,1)S(1)} collective-permute-done((bf16[1024,128]{1,0:T(8,128)(2,1)S(1)}, bf16[1024,128]{1,0:T(8,128)(2,1)S(1)}, u32[]{:S(2)}, u32[]{:S(2)}) %collective-permute-start.4) | collective-permute-done | bytes 262176 | tf_op jit(solution)/shard_map/ppermute | solution.py:358
  35.1 0.7 copy-done.4
  35.8 1.0 %copy-done.2 = f32[1024,128]{1,0:T(8,128)S(1)} copy-done((f32[1024,128]{1,0:T(8,128)S(1)}, f32[1024,128]{1,0:T(8,128)}, u32[]{:S(2)}) %copy-start.2) | copy-done | bytes 524312
  36.8 0.9 %copy-done.5 = bf16[1024,128]{1,0:T(8,128)(2,1)S(1)} copy-done((bf16[1024,128]{1,0:T(8,128)(2,1)S(1)}, bf16[1024,128]{1,0:T(8,128)(2,1)}, u32[]{:S(2)}) %copy-start.5) | copy-done | bytes 262168
  37.8 0.7 mix_rows.1
  38.5 0.7 copy-done.7
  39.2 4.9 %all-to-all-done = bf16[8,8,16,128]{3,2,1,0:T(8,128)(2,1)S(1)} async-done(((bf16[8,8,16,128]{3,2,1,0:T(8,128)(2,1)}), bf16[8,8,16,128]{3,2,1,0:T(8,128)(2,1)S(1)}, u32[]{:S(2)}, u32[]{:S(2)}) %all-to-all-start) | async-done | bytes 262176 | tf_op jit(solution)/shard_map/all_to_all | solution.py:401
  44.1 1.1 %gate.1 = bf16[4,16,16,128]{3,2,1,0:T(8,128)(2,1)} custom-call(f32[2064,128]{1,0:T(8,128)S(1)} %get-tuple-element.41.kept_ref, bf16[1,2064,128]{2,1,0:T(8,128)(2,1)S(1)} %bitcast.23, f32[3,128]{1,0:T(4,128)S(1)} %reshape.18.taps_ref), custom_call_target="tpu_custom_call" | custom-call | flops 1 | bytes 1 | tf_op jit(solution)/shard_map/gate/pallas_call | solution.py:232
  45.2 3.9 %all-to-all-start.1 = ((bf16[4,16,16,128]{3,2,1,0:T(8,128)(2,1)}), bf16[4,16,16,128]{3,2,1,0:T(8,128)(2,1)S(1)}, u32[]{:S(2)}, u32[]{:S(2)}) async-start(bf16[4,16,16,128]{3,2,1,0:T(8,128)(2,1)} %gate.1), calls=%async_computation.1 | async-start | bytes 524288 | tf_op jit(solution)/shard_map/all_to_all | solution.py:409
  49.1 1.5 %collective-permute-start.7 = (bf16[1040,128]{1,0:T(8,128)(2,1)}, bf16[1040,128]{1,0:T(8,128)(2,1)S(1)}, u32[]{:S(2)}, u32[]{:S(2)}) collective-permute-start(bf16[1040,128]{1,0:T(8,128)(2,1)} %bitcast.26), channel_id=1, source_target_pairs={{0,2},{2,0},{1,3},{3,1},{4,6},{6,4},{5,7},{7,5},{8,10},{10,8},{9,1... | collective-permute-start | bytes 798728 | tf_op jit(solution)/shard_map/ppermute | solution.py:358
  50.7 6.1 %collective-permute-done.7 = bf16[1040,128]{1,0:T(8,128)(2,1)S(1)} collective-permute-done((bf16[1040,128]{1,0:T(8,128)(2,1)}, bf16[1040,128]{1,0:T(8,128)(2,1)S(1)}, u32[]{:S(2)}, u32[]{:S(2)}) %collective-permute-start.7) | collective-permute-done | bytes 266272 | tf_op jit(solution)/shard_map/ppermute | solution.py:358
  56.7 0.8 all-to-all-done.1
  57.6 12.4 %long_conv.1 = bf16[1024,128]{1,0:T(8,128)(2,1)} custom-call(bf16[1024,128]{1,0:T(8,128)(2,1)S(1)} %bitcast.22, bf16[1024,128]{1,0:T(8,128)(2,1)S(1)} %bitcast.21, f32[1,16]{1,0:T(1,128)S(1)} %dynamic-slice_bitcast_fusion.3.bias_ref), custom_call_target="tpu_custom_call" | custom-call | flops 1 | bytes 1 | tf_op jit(solution)/shard_map/long_conv/pallas_call | solution.py:317
  69.9 5.0 %all-to-all-start.2 = ((bf16[8,8,16,128]{3,2,1,0:T(8,128)(2,1)}), bf16[8,8,16,128]{3,2,1,0:T(8,128)(2,1)S(1)}, u32[]{:S(2)}, u32[]{:S(2)}) async-start(bf16[8,8,16,128]{3,2,1,0:T(8,128)(2,1)} %bitcast.14), calls=%async_computation.2 | async-start | bytes 524288 | tf_op jit(solution)/shard_map/all_to_all | solution.py:414
  74.9 8.2 %all-to-all-done.2.z_ref = bf16[8,8,16,128]{3,2,1,0:T(8,128)(2,1)S(1)} async-done(((bf16[8,8,16,128]{3,2,1,0:T(8,128)(2,1)}), bf16[8,8,16,128]{3,2,1,0:T(8,128)(2,1)S(1)}, u32[]{:S(2)}, u32[]{:S(2)}) %all-to-all-start.2) | async-done | bytes 262176 | tf_op jit(solution)/shard_map/all_to_all | solution.py:414
  83.1 1.0 %finish.1 = bf16[1024,128]{1,0:T(8,128)(2,1)} custom-call(f32[1040,128]{1,0:T(8,128)S(1)} %get-tuple-element.40.kept_ref, bf16[1,1040,128]{2,1,0:T(8,128)(2,1)S(1)} %bitcast.24, f32[3,128]{1,0:T(4,128)S(1)} %bitcast.25, bf16[8,8,16,128]{3,2,1,0:T(8,128)(2,1)S(1)} %all-to-all-done.2.z_ref), custom_call_target="tpu_custom_call" | custom-call | flops 1 | bytes 1 | tf_op jit(solution)/shard_map/finish/pallas_call | solution.py:344
  (28 shorter events, 0.7 us)
Async XLA Ops:
  0.0 50.6 %copy-start = (f32[128]{0:T(128)S(1)}, f32[128]{0:T(128)}, u32[]{:S(2)}) copy-start(f32[128]{0:T(128)} %param.9) | copy-start | bytes 1540
  2.9 9.9 %collective-permute-start = (bf16[2048,384]{1,0:T(8,128)(2,1)}, bf16[2048,384]{1,0:T(8,128)(2,1)S(1)}, u32[]{:S(2)}, u32[]{:S(2)}) collective-permute-start(bf16[2048,384]{1,0:T(8,128)(2,1)} %pad_maximum_fusion), channel_id=1, source_target_pairs={{0,1},{1,0},{2,3},{3,2},{4,5},{5,4},{6,7},{7,6},{8,9},{9,8},{10,11... | collective-permute-start | bytes 4718600 | tf_op jit(solution)/shard_map/ppermute | solution.py:358
  4.2 13.7 %collective-permute-start.1 = (bf16[16,2048]{1,0:T(8,128)(2,1)S(1)}, bf16[16,2048]{1,0:T(8,128)(2,1)S(1)}, u32[]{:S(2)}, u32[]{:S(2)}) collective-permute-start(bf16[16,2048]{1,0:T(8,128)(2,1)S(1)} %slice.16), channel_id=1, source_target_pairs={{0,4},{4,8},{8,12},{1,5},{5,9},{9,13},{2,6},{6,10},{10,14},{3,7},{... | collective-permute-start | bytes 196616 | tf_op jit(solution)/shard_map/ppermute | solution.py:387
  17.1 0.8 copy-start.1
  22.6 4.4 %copy-start.6 = (bf16[1040,128]{1,0:T(8,128)(2,1)}, bf16[1040,128]{1,0:T(8,128)(2,1)S(1)}, u32[]{:S(2)}) copy-start(bf16[1040,128]{1,0:T(8,128)(2,1)S(1)} %get-tuple-element.39) | copy-start | bytes 798724
  22.6 5.9 %copy-start.3 = (bf16[1024,128]{1,0:T(8,128)(2,1)S(1)}, bf16[1024,128]{1,0:T(8,128)(2,1)}, u32[]{:S(2)}) copy-start(bf16[1024,128]{1,0:T(8,128)(2,1)} %h_ref) | copy-start | bytes 786436
  22.6 11.1 %copy-start.8 = (f32[3,3,128]{2,1,0:T(4,128)S(1)}, f32[3,3,128]{2,1,0:T(4,128)}, u32[]{:S(2)}) copy-start(f32[3,3,128]{2,1,0:T(4,128)} %param.7) | copy-start | bytes 13828
  22.6 2.7 %collective-permute-start.3 = (bf16[2,1040,128]{2,1,0:T(8,128)(2,1)S(1)}, bf16[2,1040,128]{2,1,0:T(8,128)(2,1)S(1)}, u32[]{:S(2)}, u32[]{:S(2)}) collective-permute-start(bf16[2,1040,128]{2,1,0:T(8,128)(2,1)S(1)} %get-tuple-element.35), channel_id=1, source_target_pairs={{0,1},{1,0},{2,3},{3,2},{4,5},{5,4},{6,7},{7,6},{8,9},{9,8},{10,11... | collective-permute-start | bytes 1597448 | tf_op jit(solution)/shard_map/ppermute | solution.py:358
  22.9 2.4 %collective-permute-start.2 = (bf16[2,1024,128]{2,1,0:T(8,128)(2,1)S(1)}, bf16[2,1024,128]{2,1,0:T(8,128)(2,1)S(1)}, u32[]{:S(2)}, u32[]{:S(2)}) collective-permute-start(bf16[2,1024,128]{2,1,0:T(8,128)(2,1)S(1)} %get-tuple-element.33), channel_id=1, source_target_pairs={{0,1},{1,0},{2,3},{3,2},{4,5},{5,4},{6,7},{7,6},{8,9},{9,8},{10,11... | collective-permute-start | bytes 1572872 | tf_op jit(solution)/shard_map/ppermute | solution.py:358
  27.0 17.2 %collective-permute-start.6 = (bf16[2064,128]{1,0:T(8,128)(2,1)}, bf16[2064,128]{1,0:T(8,128)(2,1)S(1)}, u32[]{:S(2)}, u32[]{:S(2)}) collective-permute-start(bf16[2064,128]{1,0:T(8,128)(2,1)} %bitcast.6), channel_id=1, source_target_pairs={{0,2},{2,0},{1,3},{3,1},{4,6},{6,4},{5,7},{7,5},{8,10},{10,8},{9,1... | collective-permute-start | bytes 1585160 | tf_op jit(solution)/shard_map/ppermute | solution.py:358
  28.5 46.4 %slice-start = ((f32[3,3,128]{2,1,0:T(4,128)}), f32[3,1,128]{2,1,0:T(1,128)S(1)}, s32[]{:S(2)}) async-start(f32[3,3,128]{2,1,0:T(4,128)} %param.7), calls=%async_computation.3 | async-start | bytes 3072 | tf_op jit(solution)/shard_map/slice | solution.py:415
  29.3 14.8 %all-to-all-start = ((bf16[8,8,16,128]{3,2,1,0:T(8,128)(2,1)}), bf16[8,8,16,128]{3,2,1,0:T(8,128)(2,1)S(1)}, u32[]{:S(2)}, u32[]{:S(2)}) async-start(bf16[8,8,16,128]{3,2,1,0:T(8,128)(2,1)} %filter_blocks.1), calls=%async_computation | async-start | bytes 524288 | tf_op jit(solution)/shard_map/all_to_all | solution.py:401
  33.2 2.6 %collective-permute-start.5 = (bf16[1040,128]{1,0:T(8,128)(2,1)}, bf16[1040,128]{1,0:T(8,128)(2,1)S(1)}, u32[]{:S(2)}, u32[]{:S(2)}) collective-permute-start(bf16[1040,128]{1,0:T(8,128)(2,1)} %copy-done.6), channel_id=1, source_target_pairs={{0,1},{1,0},{2,3},{3,2},{4,5},{5,4},{6,7},{7,6},{8,9},{9,8},{10,11... | collective-permute-start | bytes 798728 | tf_op jit(solution)/shard_map/ppermute | solution.py:358
  33.2 1.9 %collective-permute-start.4 = (bf16[1024,128]{1,0:T(8,128)(2,1)S(1)}, bf16[1024,128]{1,0:T(8,128)(2,1)S(1)}, u32[]{:S(2)}, u32[]{:S(2)}) collective-permute-start(bf16[1024,128]{1,0:T(8,128)(2,1)S(1)} %get-tuple-element.37), channel_id=1, source_target_pairs={{0,1},{1,0},{2,3},{3,2},{4,5},{5,4},{6,7},{7,6},{8,9},{9,8},{10,11... | collective-permute-start | bytes 786440 | tf_op jit(solution)/shard_map/ppermute | solution.py:358
  35.1 0.7 copy-start.4
  35.8 1.0 %copy-start.2 = (f32[1024,128]{1,0:T(8,128)S(1)}, f32[1024,128]{1,0:T(8,128)}, u32[]{:S(2)}) copy-start(f32[1024,128]{1,0:T(8,128)} %copy-done.1) | copy-start | bytes 1572868
  36.8 0.9 %copy-start.5 = (bf16[1024,128]{1,0:T(8,128)(2,1)S(1)}, bf16[1024,128]{1,0:T(8,128)(2,1)}, u32[]{:S(2)}) copy-start(bf16[1024,128]{1,0:T(8,128)(2,1)} %copy-done.4) | copy-start | bytes 786436
  38.5 0.7 copy-start.7
  45.2 12.3 %all-to-all-start.1 = ((bf16[4,16,16,128]{3,2,1,0:T(8,128)(2,1)}), bf16[4,16,16,128]{3,2,1,0:T(8,128)(2,1)S(1)}, u32[]{:S(2)}, u32[]{:S(2)}) async-start(bf16[4,16,16,128]{3,2,1,0:T(8,128)(2,1)} %gate.1), calls=%async_computation.1 | async-start | bytes 524288 | tf_op jit(solution)/shard_map/all_to_all | solution.py:409
  49.1 7.6 %collective-permute-start.7 = (bf16[1040,128]{1,0:T(8,128)(2,1)}, bf16[1040,128]{1,0:T(8,128)(2,1)S(1)}, u32[]{:S(2)}, u32[]{:S(2)}) collective-permute-start(bf16[1040,128]{1,0:T(8,128)(2,1)} %bitcast.26), channel_id=1, source_target_pairs={{0,2},{2,0},{1,3},{3,1},{4,6},{6,4},{5,7},{7,5},{8,10},{10,8},{9,1... | collective-permute-start | bytes 798728 | tf_op jit(solution)/shard_map/ppermute | solution.py:358
  69.9 13.2 %all-to-all-start.2 = ((bf16[8,8,16,128]{3,2,1,0:T(8,128)(2,1)}), bf16[8,8,16,128]{3,2,1,0:T(8,128)(2,1)S(1)}, u32[]{:S(2)}, u32[]{:S(2)}) async-start(bf16[8,8,16,128]{3,2,1,0:T(8,128)(2,1)} %bitcast.14), calls=%async_computation.2 | async-start | bytes 524288 | tf_op jit(solution)/shard_map/all_to_all | solution.py:414

commit v3 on v2

--- a/solution.py
+++ b/solution.py
@@ -40,9 +40,9 @@
 
 def project_body(place_ref, tok_ref, *refs, halo):
     if halo:
-        halo_ref, w_ref, other_ref, kv_own, kv_away, q_own, q_away, own_w, query_w, sems = refs
+        halo_ref, w_ref, other_ref, kv_own, kv_away, q_own, q_away, own_w, other_w, query_w, sems = refs
     else:
-        w_ref, other_ref, kv_own, kv_away, q_own, q_away, own_w, query_w, sems = refs
+        w_ref, other_ref, kv_own, kv_away, q_own, q_away, own_w, other_w, query_w, sems = refs
     rows, depth = tok_ref.shape
     width = w_ref.shape[2]
     start = place_ref[1] * depth
@@ -68,8 +68,10 @@
         q_own[at : at + product.shape[0], :] = product[:, :width]
         q_away[at : at + product.shape[0], :] = product[:, width:].astype(bf16)
 
-    passes(other_ref[:, : 2 * width], lambda product, at: spread(kv_away, product, at, width))
-    query_w[:, width:] = other_ref[:, 2 * width :]
+    other_w[:, :width] = other_ref[1]
+    other_w[:, width:] = other_ref[2]
+    passes(other_w[...], lambda product, at: spread(kv_away, product, at, width))
+    query_w[:, width:] = other_ref[0]
     for copy in copies:
         copy.wait()
     passes(own_w[...], lambda product, at: spread(kv_own, product, at, width))
@@ -97,6 +99,7 @@
         scratch_shapes=[
             pltpu.VMEM((depth, 2 * width), bf16),
             pltpu.VMEM((depth, 2 * width), bf16),
+            pltpu.VMEM((depth, 2 * width), bf16),
             pltpu.SemaphoreType.DMA((3,)),
         ],
         compiler_params=params(14),
@@ -379,11 +382,7 @@
 
     w = w_proj.transpose(1, 0, 2)
     w_hbm = pltpu.with_memory_space_constraint(w, pltpu.HBM)
-    theirs = [
-        lax.dynamic_slice(w, (pick, (1 - c) * depth, 0), (1, depth, channels))[0]
-        for pick in (1, 2, 0)
-    ]
-    other = swap(jnp.concatenate(theirs, axis=1), "chan")
+    other = swap(lax.dynamic_slice_in_dim(w, (1 - c) * depth, depth, 1), "chan")
     halo = lax.ppermute(tokens[rows - HALO :], "seq", [(i, i + 1) for i in range(n_seq - 1)])
 
     half = rows // 2

time: 84.7 us -> 84.7 us (level)
  other arithmetic: 1.48 us -> 0.08 us
  local copies, waits for them, and re-layouts: 10.8 us -> 12 us
    dynamic_slice x0 -> x1, local copies, waits for them, and re-layouts: none -> 2.71 us  [shards(): other = swap(lax.dynamic_slice_in_dim(w, (1 - c) * depth, depth, 1), 'chan')]
    squeeze x1 -> x0, local copies, waits for them, and re-layouts: 1.47 us -> none  [shards(): lax.dynamic_slice(w, (pick, (1 - c) * depth, 0), (1, depth, channels))[0]]
    concatenate x1 -> x0, other arithmetic: 1.41 us -> none  [shards(): other = swap(jnp.concatenate(theirs, axis=1), 'chan')]
where the time goes in v3:
time: 84.7 us; the launch traced here: 84.1 us
  Pallas kernels  26.8 us (32%)
  waiting for transfers between devices  23.3 us (28%)
  starting transfers between devices  21.7 us (26%)
  local copies, waits for them, and re-layouts  12 us (14%)
    pallas_call x1, Pallas kernels, long_conv(): pl.pallas_call(functools.partial(conv_body, chans=chans, blocks=blocks),...  12.4 us
    ppermute x7, waiting for transfers between devices, swap(): lax.ppermute(array, axis, [(i, (i + by) % size) for i in range(size)])  9.46 us
    pallas_call x2, Pallas kernels, project(): pl.pallas_call(functools.partial(project_body, halo=halo is not None), ou...  9.22 us
    all_to_all x1, waiting for transfers between devices, shards(): z = lax.all_to_all(z, RING, split_axis=0, concat_axis=0, tiled=True)  8.21 us
    all_to_all x1, starting transfers between devices, shards(): z = lax.all_to_all(z, RING, split_axis=0, concat_axis=0, tiled=True)  4.95 us
    all_to_all x1, waiting for transfers between devices, shards(): filt = lax.all_to_all(filt, RING, split_axis=0, concat_axis=0, tiled=True)  4.86 us
    ppermute x7, starting transfers between devices, swap(): lax.ppermute(array, axis, [(i, (i + by) % size) for i in range(size)])  4.52 us
    ppermute x1, starting transfers between devices, shards(): lax.ppermute(tokens[rows - HALO:], 'seq', [(i, i + 1) for i in range(n_se...  4.47 us
  transfers between devices with their start and end apart: 11, of which 6 were waited for; matrix products, arithmetic and copies ran while one was open for 6% of the time, Pallas kernels for 7%

profile of v3, /device:TPU:0, one launch (start us, length us, event | category | flops | bytes accessed | tf_op | source)
XLA Modules:
  0.0 84.1 jit_solution(9569129649355867163)
XLA Ops:
  0.0 2.7 %dynamic-slice_bitcast_fusion = bf16[3,2048,128]{2,1,0:T(8,128)(2,1)} fusion(bf16[4096,3,128]{2,0,1:T(8,128)(2,1)} %param.6, s32[]{:T(128)S(6)} %select_n.9), kind=kLoop, calls=%fused_computation | loop fusion | bytes 3145732 | tf_op jit(solution)/shard_map/dynamic_slice | solution.py:385
  2.7 0.5 collective-permute-start
  3.2 0.8 %slice.16 = bf16[16,2048]{1,0:T(8,128)(2,1)S(1)} slice(bf16[2048,2048]{1,0:T(8,128)(2,1)} %param.5), slice={[2032:2048], [0:2048]} | slice | bytes 131072 | tf_op jit(solution)/shard_map/slice | solution.py:386
  4.0 4.5 %collective-permute-start.1 = (bf16[16,2048]{1,0:T(8,128)(2,1)S(1)}, bf16[16,2048]{1,0:T(8,128)(2,1)S(1)}, u32[]{:S(2)}, u32[]{:S(2)}) collective-permute-start(bf16[16,2048]{1,0:T(8,128)(2,1)S(1)} %slice.16), channel_id=1, source_target_pairs={{0,4},{4,8},{8,12},{1,5},{5,9},{9,13},{2,6},{6,10},{10,14},{3,7},{... | collective-permute-start | bytes 196616 | tf_op jit(solution)/shard_map/ppermute | solution.py:386
  8.5 4.0 %fusion = (bf16[1024,2048]{1,0:T(8,128)(2,1)S(1)}, bf16[1024,2048]{1,0:T(8,128)(2,1)S(1)}) fusion(bf16[2048,2048]{1,0:T(8,128)(2,1)} %param.5), kind=kLoop, calls=%fused_computation.5 | loop fusion | bytes 16777216 | tf_op jit(solution)/shard_map/slice | solution.py:392
  12.6 4.4 %project.2 = (f32[2,1024,128]{2,1,0:T(8,128)S(1)}, bf16[2,1024,128]{2,1,0:T(8,128)(2,1)S(1)}, f32[1024,128]{1,0:T(8,128)S(1)}, bf16[1024,128]{1,0:T(8,128)(2,1)S(1)}) custom-call(s32[2]{0:T(128)S(1)} %pad_add_fusion.place_ref, bf16[1024,2048]{1,0:T(8,128)(2,1)S(1)} %get-tuple-element.50.tok_ref, bf16[3,4096,128]{2,1,0:T(8,128)(2,1)} %bitcast.23, ...), custom_call_target="tpu_custom_call" | custom-call | flops 1 | bytes 1 | tf_op jit(solution)/shard_map/project/pallas_call | solution.py:87
  17.0 0.8 copy-done.1
  17.8 4.8 %project.3 = (f32[2,1040,128]{2,1,0:T(8,128)S(1)}, bf16[2,1040,128]{2,1,0:T(8,128)(2,1)S(1)}, f32[1040,128]{1,0:T(8,128)S(1)}, bf16[1040,128]{1,0:T(8,128)(2,1)S(1)}) custom-call(s32[2]{0:T(128)S(1)} %pad_add_fusion.place_ref, bf16[1024,2048]{1,0:T(8,128)(2,1)S(1)} %get-tuple-element.49.tok_ref, bf16[16,2048]{1,0:T(8,128)(2,1)S(1)} %collective-permute-done.1.refs_0_, ...), custom_call_target="tpu_custom_call" | custom-call | flops 1 | bytes 1 | tf_op jit(solution)/shard_map/project/pallas_call | solution.py:87
  22.7 0.3 collective-permute-start.3
  22.9 0.3 collective-permute-start.2
  23.2 2.2 %collective-permute-done.2.came_a = bf16[2,1024,128]{2,1,0:T(8,128)(2,1)S(1)} collective-permute-done((bf16[2,1024,128]{2,1,0:T(8,128)(2,1)S(1)}, bf16[2,1024,128]{2,1,0:T(8,128)(2,1)S(1)}, u32[]{:S(2)}, u32[]{:S(2)}) %collective-permute-start.2) | collective-permute-done | bytes 524320 | tf_op jit(solution)/shard_map/ppermute | solution.py:361
  25.4 1.6 %mix.1 = (f32[2064,128]{1,0:T(8,128)S(1)}, bf16[1,2064,128]{2,1,0:T(8,128)(2,1)}) custom-call(s32[2]{0:T(128)S(1)} %pad_add_fusion.place_ref, f32[2,1024,128]{2,1,0:T(8,128)S(1)} %get-tuple-element.32.own_a, bf16[2,1024,128]{2,1,0:T(8,128)(2,1)S(1)} %collective-permute-done.2.came_a, f32[2,1040,128]{2,1,0:T(8,128)S(1)} %get-tuple-element.34.own_b, ...), custom_call_target="tpu_custom_call" | custom-call | flops 1 | bytes 1 | tf_op jit(solution)/shard_map/mix/pallas_call | solution.py:136
  27.0 1.5 %collective-permute-start.6 = (bf16[2064,128]{1,0:T(8,128)(2,1)}, bf16[2064,128]{1,0:T(8,128)(2,1)S(1)}, u32[]{:S(2)}, u32[]{:S(2)}) collective-permute-start(bf16[2064,128]{1,0:T(8,128)(2,1)} %bitcast.4), channel_id=1, source_target_pairs={{0,2},{2,0},{1,3},{3,1},{4,6},{6,4},{5,7},{7,5},{8,10},{10,8},{9,1... | collective-permute-start | bytes 1585160 | tf_op jit(solution)/shard_map/ppermute | solution.py:361
  28.5 0.8 %filter_blocks.1 = bf16[8,8,16,128]{3,2,1,0:T(8,128)(2,1)} custom-call(bf16[1024,128]{1,0:T(8,128)(2,1)S(1)} %copy-done.3), custom_call_target="tpu_custom_call" | custom-call | flops 1 | bytes 1 | tf_op jit(solution)/shard_map/filter_blocks/pallas_call | solution.py:199
  29.3 3.9 %all-to-all-start = ((bf16[8,8,16,128]{3,2,1,0:T(8,128)(2,1)}), bf16[8,8,16,128]{3,2,1,0:T(8,128)(2,1)S(1)}, u32[]{:S(2)}, u32[]{:S(2)}) async-start(bf16[8,8,16,128]{3,2,1,0:T(8,128)(2,1)} %filter_blocks.1), calls=%async_computation | async-start | bytes 524288 | tf_op jit(solution)/shard_map/all_to_all | solution.py:400
  33.2 0.5 collective-permute-start.4
  33.9 1.2 %collective-permute-done.4.came_a = bf16[1024,128]{1,0:T(8,128)(2,1)S(1)} collective-permute-done((bf16[1024,128]{1,0:T(8,128)(2,1)S(1)}, bf16[1024,128]{1,0:T(8,128)(2,1)S(1)}, u32[]{:S(2)}, u32[]{:S(2)}) %collective-permute-start.4) | collective-permute-done | bytes 262176 | tf_op jit(solution)/shard_map/ppermute | solution.py:361
  35.1 0.7 copy-done.4
  35.8 1.0 %copy-done.2 = f32[1024,128]{1,0:T(8,128)S(1)} copy-done((f32[1024,128]{1,0:T(8,128)S(1)}, f32[1024,128]{1,0:T(8,128)}, u32[]{:S(2)}) %copy-start.2) | copy-done | bytes 524312
  36.9 0.9 %copy-done.5 = bf16[1024,128]{1,0:T(8,128)(2,1)S(1)} copy-done((bf16[1024,128]{1,0:T(8,128)(2,1)S(1)}, bf16[1024,128]{1,0:T(8,128)(2,1)}, u32[]{:S(2)}) %copy-start.5) | copy-done | bytes 262168
  37.8 0.7 mix_rows.1
  38.6 0.7 copy-done.7
  39.3 4.9 %all-to-all-done = bf16[8,8,16,128]{3,2,1,0:T(8,128)(2,1)S(1)} async-done(((bf16[8,8,16,128]{3,2,1,0:T(8,128)(2,1)}), bf16[8,8,16,128]{3,2,1,0:T(8,128)(2,1)S(1)}, u32[]{:S(2)}, u32[]{:S(2)}) %all-to-all-start) | async-done | bytes 262176 | tf_op jit(solution)/shard_map/all_to_all | solution.py:400
  44.1 1.1 %gate.1 = bf16[4,16,16,128]{3,2,1,0:T(8,128)(2,1)} custom-call(f32[2064,128]{1,0:T(8,128)S(1)} %get-tuple-element.41.kept_ref, bf16[1,2064,128]{2,1,0:T(8,128)(2,1)S(1)} %bitcast.19, f32[3,128]{1,0:T(4,128)S(1)} %reshape.12.taps_ref), custom_call_target="tpu_custom_call" | custom-call | flops 1 | bytes 1 | tf_op jit(solution)/shard_map/gate/pallas_call | solution.py:235
  45.3 3.9 %all-to-all-start.1 = ((bf16[4,16,16,128]{3,2,1,0:T(8,128)(2,1)}), bf16[4,16,16,128]{3,2,1,0:T(8,128)(2,1)S(1)}, u32[]{:S(2)}, u32[]{:S(2)}) async-start(bf16[4,16,16,128]{3,2,1,0:T(8,128)(2,1)} %gate.1), calls=%async_computation.1 | async-start | bytes 524288 | tf_op jit(solution)/shard_map/all_to_all | solution.py:408
  49.1 1.5 %collective-permute-start.7 = (bf16[1040,128]{1,0:T(8,128)(2,1)}, bf16[1040,128]{1,0:T(8,128)(2,1)S(1)}, u32[]{:S(2)}, u32[]{:S(2)}) collective-permute-start(bf16[1040,128]{1,0:T(8,128)(2,1)} %bitcast.22), channel_id=1, source_target_pairs={{0,2},{2,0},{1,3},{3,1},{4,6},{6,4},{5,7},{7,5},{8,10},{10,8},{9,1... | collective-permute-start | bytes 798728 | tf_op jit(solution)/shard_map/ppermute | solution.py:361
  50.7 6.0 %collective-permute-done.7 = bf16[1040,128]{1,0:T(8,128)(2,1)S(1)} collective-permute-done((bf16[1040,128]{1,0:T(8,128)(2,1)}, bf16[1040,128]{1,0:T(8,128)(2,1)S(1)}, u32[]{:S(2)}, u32[]{:S(2)}) %collective-permute-start.7) | collective-permute-done | bytes 266272 | tf_op jit(solution)/shard_map/ppermute | solution.py:361
  56.7 0.8 all-to-all-done.1
  57.5 12.4 %long_conv.1 = bf16[1024,128]{1,0:T(8,128)(2,1)} custom-call(bf16[1024,128]{1,0:T(8,128)(2,1)S(1)} %bitcast.18, bf16[1024,128]{1,0:T(8,128)(2,1)S(1)} %bitcast.17, f32[1,16]{1,0:T(1,128)S(1)} %dynamic-slice_bitcast_fusion.1.bias_ref), custom_call_target="tpu_custom_call" | custom-call | flops 1 | bytes 1 | tf_op jit(solution)/shard_map/long_conv/pallas_call | solution.py:320
  69.9 5.0 %all-to-all-start.2 = ((bf16[8,8,16,128]{3,2,1,0:T(8,128)(2,1)}), bf16[8,8,16,128]{3,2,1,0:T(8,128)(2,1)S(1)}, u32[]{:S(2)}, u32[]{:S(2)}) async-start(bf16[8,8,16,128]{3,2,1,0:T(8,128)(2,1)} %bitcast.12), calls=%async_computation.2 | async-start | bytes 524288 | tf_op jit(solution)/shard_map/all_to_all | solution.py:413
  74.9 8.2 %all-to-all-done.2.z_ref = bf16[8,8,16,128]{3,2,1,0:T(8,128)(2,1)S(1)} async-done(((bf16[8,8,16,128]{3,2,1,0:T(8,128)(2,1)}), bf16[8,8,16,128]{3,2,1,0:T(8,128)(2,1)S(1)}, u32[]{:S(2)}, u32[]{:S(2)}) %all-to-all-start.2) | async-done | bytes 262176 | tf_op jit(solution)/shard_map/all_to_all | solution.py:413
  83.1 1.0 %finish.1 = bf16[1024,128]{1,0:T(8,128)(2,1)} custom-call(f32[1040,128]{1,0:T(8,128)S(1)} %get-tuple-element.40.kept_ref, bf16[1,1040,128]{2,1,0:T(8,128)(2,1)S(1)} %bitcast.20, f32[3,128]{1,0:T(4,128)S(1)} %bitcast.21, bf16[8,8,16,128]{3,2,1,0:T(8,128)(2,1)S(1)} %all-to-all-done.2.z_ref), custom_call_target="tpu_custom_call" | custom-call | flops 1 | bytes 1 | tf_op jit(solution)/shard_map/finish/pallas_call | solution.py:347
  (27 shorter events, 0.4 us)
Async XLA Ops:
  0.0 50.6 %copy-start = (f32[128]{0:T(128)S(1)}, f32[128]{0:T(128)}, u32[]{:S(2)}) copy-start(f32[128]{0:T(128)} %param.9) | copy-start | bytes 1540
  2.7 9.9 %collective-permute-start = (bf16[3,2048,128]{2,1,0:T(8,128)(2,1)}, bf16[3,2048,128]{2,1,0:T(8,128)(2,1)S(1)}, u32[]{:S(2)}, u32[]{:S(2)}) collective-permute-start(bf16[3,2048,128]{2,1,0:T(8,128)(2,1)} %dynamic-slice_bitcast_fusion), channel_id=1, source_target_pairs={{0,1},{1,0},{2,3},{3,2},{4,5},{5,4},{6,7},{7,6},{8,9},{9,8},{10,11... | collective-permute-start | bytes 4718600 | tf_op jit(solution)/shard_map/ppermute | solution.py:361
  4.0 13.8 %collective-permute-start.1 = (bf16[16,2048]{1,0:T(8,128)(2,1)S(1)}, bf16[16,2048]{1,0:T(8,128)(2,1)S(1)}, u32[]{:S(2)}, u32[]{:S(2)}) collective-permute-start(bf16[16,2048]{1,0:T(8,128)(2,1)S(1)} %slice.16), channel_id=1, source_target_pairs={{0,4},{4,8},{8,12},{1,5},{5,9},{9,13},{2,6},{6,10},{10,14},{3,7},{... | collective-permute-start | bytes 196616 | tf_op jit(solution)/shard_map/ppermute | solution.py:386
  17.0 0.8 copy-start.1
  22.6 4.3 %copy-start.6 = (bf16[1040,128]{1,0:T(8,128)(2,1)}, bf16[1040,128]{1,0:T(8,128)(2,1)S(1)}, u32[]{:S(2)}) copy-start(bf16[1040,128]{1,0:T(8,128)(2,1)S(1)} %get-tuple-element.39) | copy-start | bytes 798724
  22.6 5.8 %copy-start.3 = (bf16[1024,128]{1,0:T(8,128)(2,1)S(1)}, bf16[1024,128]{1,0:T(8,128)(2,1)}, u32[]{:S(2)}) copy-start(bf16[1024,128]{1,0:T(8,128)(2,1)} %h_ref) | copy-start | bytes 786436
  22.7 11.1 %copy-start.8 = (f32[3,3,128]{2,1,0:T(4,128)S(1)}, f32[3,3,128]{2,1,0:T(4,128)}, u32[]{:S(2)}) copy-start(f32[3,3,128]{2,1,0:T(4,128)} %param.7) | copy-start | bytes 13828
  22.7 2.7 %collective-permute-start.3 = (bf16[2,1040,128]{2,1,0:T(8,128)(2,1)S(1)}, bf16[2,1040,128]{2,1,0:T(8,128)(2,1)S(1)}, u32[]{:S(2)}, u32[]{:S(2)}) collective-permute-start(bf16[2,1040,128]{2,1,0:T(8,128)(2,1)S(1)} %get-tuple-element.35), channel_id=1, source_target_pairs={{0,1},{1,0},{2,3},{3,2},{4,5},{5,4},{6,7},{7,6},{8,9},{9,8},{10,11... | collective-permute-start | bytes 1597448 | tf_op jit(solution)/shard_map/ppermute | solution.py:361
  22.9 2.5 %collective-permute-start.2 = (bf16[2,1024,128]{2,1,0:T(8,128)(2,1)S(1)}, bf16[2,1024,128]{2,1,0:T(8,128)(2,1)S(1)}, u32[]{:S(2)}, u32[]{:S(2)}) collective-permute-start(bf16[2,1024,128]{2,1,0:T(8,128)(2,1)S(1)} %get-tuple-element.33), channel_id=1, source_target_pairs={{0,1},{1,0},{2,3},{3,2},{4,5},{5,4},{6,7},{7,6},{8,9},{9,8},{10,11... | collective-permute-start | bytes 1572872 | tf_op jit(solution)/shard_map/ppermute | solution.py:361
  27.0 17.2 %collective-permute-start.6 = (bf16[2064,128]{1,0:T(8,128)(2,1)}, bf16[2064,128]{1,0:T(8,128)(2,1)S(1)}, u32[]{:S(2)}, u32[]{:S(2)}) collective-permute-start(bf16[2064,128]{1,0:T(8,128)(2,1)} %bitcast.4), channel_id=1, source_target_pairs={{0,2},{2,0},{1,3},{3,1},{4,6},{6,4},{5,7},{7,5},{8,10},{10,8},{9,1... | collective-permute-start | bytes 1585160 | tf_op jit(solution)/shard_map/ppermute | solution.py:361
  28.5 46.4 %slice-start = ((f32[3,3,128]{2,1,0:T(4,128)}), f32[3,1,128]{2,1,0:T(1,128)S(1)}, s32[]{:S(2)}) async-start(f32[3,3,128]{2,1,0:T(4,128)} %param.7), calls=%async_computation.3 | async-start | bytes 3072 | tf_op jit(solution)/shard_map/slice | solution.py:414
  29.3 14.8 %all-to-all-start = ((bf16[8,8,16,128]{3,2,1,0:T(8,128)(2,1)}), bf16[8,8,16,128]{3,2,1,0:T(8,128)(2,1)S(1)}, u32[]{:S(2)}, u32[]{:S(2)}) async-start(bf16[8,8,16,128]{3,2,1,0:T(8,128)(2,1)} %filter_blocks.1), calls=%async_computation | async-start | bytes 524288 | tf_op jit(solution)/shard_map/all_to_all | solution.py:400
  33.2 2.6 %collective-permute-start.5 = (bf16[1040,128]{1,0:T(8,128)(2,1)}, bf16[1040,128]{1,0:T(8,128)(2,1)S(1)}, u32[]{:S(2)}, u32[]{:S(2)}) collective-permute-start(bf16[1040,128]{1,0:T(8,128)(2,1)} %copy-done.6), channel_id=1, source_target_pairs={{0,1},{1,0},{2,3},{3,2},{4,5},{5,4},{6,7},{7,6},{8,9},{9,8},{10,11... | collective-permute-start | bytes 798728 | tf_op jit(solution)/shard_map/ppermute | solution.py:361
  33.2 1.9 %collective-permute-start.4 = (bf16[1024,128]{1,0:T(8,128)(2,1)S(1)}, bf16[1024,128]{1,0:T(8,128)(2,1)S(1)}, u32[]{:S(2)}, u32[]{:S(2)}) collective-permute-start(bf16[1024,128]{1,0:T(8,128)(2,1)S(1)} %get-tuple-element.37), channel_id=1, source_target_pairs={{0,1},{1,0},{2,3},{3,2},{4,5},{5,4},{6,7},{7,6},{8,9},{9,8},{10,11... | collective-permute-start | bytes 786440 | tf_op jit(solution)/shard_map/ppermute | solution.py:361
  35.1 0.7 copy-start.4
  35.8 1.0 %copy-start.2 = (f32[1024,128]{1,0:T(8,128)S(1)}, f32[1024,128]{1,0:T(8,128)}, u32[]{:S(2)}) copy-start(f32[1024,128]{1,0:T(8,128)} %copy-done.1) | copy-start | bytes 1572868
  36.9 0.9 %copy-start.5 = (bf16[1024,128]{1,0:T(8,128)(2,1)S(1)}, bf16[1024,128]{1,0:T(8,128)(2,1)}, u32[]{:S(2)}) copy-start(bf16[1024,128]{1,0:T(8,128)(2,1)} %copy-done.4) | copy-start | bytes 786436
  38.5 0.7 copy-start.7
  45.3 12.3 %all-to-all-start.1 = ((bf16[4,16,16,128]{3,2,1,0:T(8,128)(2,1)}), bf16[4,16,16,128]{3,2,1,0:T(8,128)(2,1)S(1)}, u32[]{:S(2)}, u32[]{:S(2)}) async-start(bf16[4,16,16,128]{3,2,1,0:T(8,128)(2,1)} %gate.1), calls=%async_computation.1 | async-start | bytes 524288 | tf_op jit(solution)/shard_map/all_to_all | solution.py:408
  49.1 7.6 %collective-permute-start.7 = (bf16[1040,128]{1,0:T(8,128)(2,1)}, bf16[1040,128]{1,0:T(8,128)(2,1)S(1)}, u32[]{:S(2)}, u32[]{:S(2)}) collective-permute-start(bf16[1040,128]{1,0:T(8,128)(2,1)} %bitcast.22), channel_id=1, source_target_pairs={{0,2},{2,0},{1,3},{3,1},{4,6},{6,4},{5,7},{7,5},{8,10},{10,8},{9,1... | collective-permute-start | bytes 798728 | tf_op jit(solution)/shard_map/ppermute | solution.py:361
  69.9 13.2 %all-to-all-start.2 = ((bf16[8,8,16,128]{3,2,1,0:T(8,128)(2,1)}), bf16[8,8,16,128]{3,2,1,0:T(8,128)(2,1)S(1)}, u32[]{:S(2)}, u32[]{:S(2)}) async-start(bf16[8,8,16,128]{3,2,1,0:T(8,128)(2,1)} %bitcast.12), calls=%async_computation.2 | async-start | bytes 524288 | tf_op jit(solution)/shard_map/all_to_all | solution.py:413

commit v4 on v2

--- a/solution.py
+++ b/solution.py
@@ -307,7 +307,7 @@
 def long_conv(gated, filt, bias, chans):
     rows = gated.shape[0]
     blocks = rows // chans
-    together = math.gcd(chans, 4)
+    together = math.gcd(chans, 8)
     one = [
         pltpu.VMEM((2 * blocks + GROUP, LANES), f32),
         pltpu.VMEM((blocks + 2 * GROUP, LANES), f32),

time: 84.7 us -> 84 us (level)
  no operation moved by 1% of the time
where the time goes in v4:
time: 84 us; the launch traced here: 83.5 us
  Pallas kernels  26 us (31%)
  waiting for transfers between devices  23.4 us (28%)
  starting transfers between devices  21.6 us (26%)
  local copies, waits for them, and re-layouts  10.8 us (13%)
  other arithmetic  1.48 us (2%)
    pallas_call x1, Pallas kernels, long_conv(): pl.pallas_call(functools.partial(conv_body, chans=chans, blocks=blocks),...  11.8 us
    ppermute x7, waiting for transfers between devices, swap(): lax.ppermute(array, axis, [(i, (i + by) % size) for i in range(size)])  9.55 us
    pallas_call x2, Pallas kernels, project(): pl.pallas_call(functools.partial(project_body, halo=halo is not None), ou...  9 us
    all_to_all x1, waiting for transfers between devices, shards(): z = lax.all_to_all(z, RING, split_axis=0, concat_axis=0, tiled=True)  8.21 us
    all_to_all x1, starting transfers between devices, shards(): z = lax.all_to_all(z, RING, split_axis=0, concat_axis=0, tiled=True)  4.92 us
    all_to_all x1, waiting for transfers between devices, shards(): filt = lax.all_to_all(filt, RING, split_axis=0, concat_axis=0, tiled=True)  4.87 us
    ppermute x7, starting transfers between devices, swap(): lax.ppermute(array, axis, [(i, (i + by) % size) for i in range(size)])  4.53 us
    ppermute x1, starting transfers between devices, shards(): lax.ppermute(tokens[rows - HALO:], 'seq', [(i, i + 1) for i in range(n_se...  4.47 us
  transfers between devices with their start and end apart: 11, of which 6 were waited for; matrix products, arithmetic and copies ran while one was open for 6% of the time, Pallas kernels for 7%

profile of v4, /device:TPU:0, one launch (start us, length us, event | category | flops | bytes accessed | tf_op | source)
XLA Modules:
  0.0 83.5 jit_solution(17940712575951637647)
XLA Ops:
  0.0 1.5 %dynamic-slice_bitcast_fusion.2 = (bf16[2048,128]{1,0:T(8,128)(2,1)S(1)}, bf16[2048,128]{1,0:T(8,128)(2,1)S(1)}, bf16[2048,128]{1,0:T(8,128)(2,1)S(1)}) fusion(bf16[4096,3,128]{2,0,1:T(8,128)(2,1)} %param.6, s32[]{:T(128)S(6)} %select_n.11), kind=kLoop, calls=%fused_computation.3 | loop fusion | bytes 3145732 | tf_op jit(solution)/shard_map/squeeze | solution.py:383
  1.5 1.4 %pad_maximum_fusion = bf16[2048,384]{1,0:T(8,128)(2,1)} fusion(bf16[2048,128]{1,0:T(8,128)(2,1)S(1)} %get-tuple-element.52, bf16[2048,128]{1,0:T(8,128)(2,1)S(1)} %get-tuple-element.53, bf16[2048,128]{1,0:T(8,128)(2,1)S(1)} %get-tuple-element.51), kind=kLoop, calls=%fused_computation | loop fusion | flops 4718592 | bytes 3145728 | tf_op jit(solution)/shard_map/concatenate | solution.py:386
  2.9 0.5 collective-permute-start
  3.3 0.8 %slice.16 = bf16[16,2048]{1,0:T(8,128)(2,1)S(1)} slice(bf16[2048,2048]{1,0:T(8,128)(2,1)} %param.5), slice={[2032:2048], [0:2048]} | slice | bytes 131072 | tf_op jit(solution)/shard_map/slice | solution.py:387
  4.2 4.5 %collective-permute-start.1 = (bf16[16,2048]{1,0:T(8,128)(2,1)S(1)}, bf16[16,2048]{1,0:T(8,128)(2,1)S(1)}, u32[]{:S(2)}, u32[]{:S(2)}) collective-permute-start(bf16[16,2048]{1,0:T(8,128)(2,1)S(1)} %slice.16), channel_id=1, source_target_pairs={{0,4},{4,8},{8,12},{1,5},{5,9},{9,13},{2,6},{6,10},{10,14},{3,7},{... | collective-permute-start | bytes 196616 | tf_op jit(solution)/shard_map/ppermute | solution.py:387
  8.7 4.0 %fusion = (bf16[1024,2048]{1,0:T(8,128)(2,1)S(1)}, bf16[1024,2048]{1,0:T(8,128)(2,1)S(1)}) fusion(bf16[2048,2048]{1,0:T(8,128)(2,1)} %param.5), kind=kLoop, calls=%fused_computation.8 | loop fusion | bytes 16777216 | tf_op jit(solution)/shard_map/slice | solution.py:393
  12.8 4.3 %project.2 = (f32[2,1024,128]{2,1,0:T(8,128)S(1)}, bf16[2,1024,128]{2,1,0:T(8,128)(2,1)S(1)}, f32[1024,128]{1,0:T(8,128)S(1)}, bf16[1024,128]{1,0:T(8,128)(2,1)S(1)}) custom-call(s32[2]{0:T(128)S(1)} %pad_add_fusion.place_ref, bf16[1024,2048]{1,0:T(8,128)(2,1)S(1)} %get-tuple-element.50.tok_ref, bf16[3,4096,128]{2,1,0:T(8,128)(2,1)} %bitcast.27, ...), custom_call_target="tpu_custom_call" | custom-call | flops 1 | bytes 1 | tf_op jit(solution)/shard_map/project/pallas_call | solution.py:85
  17.1 0.8 copy-done.1
  17.9 4.7 %project.3 = (f32[2,1040,128]{2,1,0:T(8,128)S(1)}, bf16[2,1040,128]{2,1,0:T(8,128)(2,1)S(1)}, f32[1040,128]{1,0:T(8,128)S(1)}, bf16[1040,128]{1,0:T(8,128)(2,1)S(1)}) custom-call(s32[2]{0:T(128)S(1)} %pad_add_fusion.place_ref, bf16[1024,2048]{1,0:T(8,128)(2,1)S(1)} %get-tuple-element.49.tok_ref, bf16[16,2048]{1,0:T(8,128)(2,1)S(1)} %collective-permute-done.1.refs_0_, ...), custom_call_target="tpu_custom_call" | custom-call | flops 1 | bytes 1 | tf_op jit(solution)/shard_map/project/pallas_call | solution.py:85
  22.6 0.3 collective-permute-start.3
  23.2 2.2 %collective-permute-done.2.came_a = bf16[2,1024,128]{2,1,0:T(8,128)(2,1)S(1)} collective-permute-done((bf16[2,1024,128]{2,1,0:T(8,128)(2,1)S(1)}, bf16[2,1024,128]{2,1,0:T(8,128)(2,1)S(1)}, u32[]{:S(2)}, u32[]{:S(2)}) %collective-permute-start.2) | collective-permute-done | bytes 524320 | tf_op jit(solution)/shard_map/ppermute | solution.py:358
  25.4 1.6 %mix.1 = (f32[2064,128]{1,0:T(8,128)S(1)}, bf16[1,2064,128]{2,1,0:T(8,128)(2,1)}) custom-call(s32[2]{0:T(128)S(1)} %pad_add_fusion.place_ref, f32[2,1024,128]{2,1,0:T(8,128)S(1)} %get-tuple-element.32.own_a, bf16[2,1024,128]{2,1,0:T(8,128)(2,1)S(1)} %collective-permute-done.2.came_a, f32[2,1040,128]{2,1,0:T(8,128)S(1)} %get-tuple-element.34.own_b, ...), custom_call_target="tpu_custom_call" | custom-call | flops 1 | bytes 1 | tf_op jit(solution)/shard_map/mix/pallas_call | solution.py:133
  27.0 1.5 %collective-permute-start.6 = (bf16[2064,128]{1,0:T(8,128)(2,1)}, bf16[2064,128]{1,0:T(8,128)(2,1)S(1)}, u32[]{:S(2)}, u32[]{:S(2)}) collective-permute-start(bf16[2064,128]{1,0:T(8,128)(2,1)} %bitcast.6), channel_id=1, source_target_pairs={{0,2},{2,0},{1,3},{3,1},{4,6},{6,4},{5,7},{7,5},{8,10},{10,8},{9,1... | collective-permute-start | bytes 1585160 | tf_op jit(solution)/shard_map/ppermute | solution.py:358
  28.5 0.8 %filter_blocks.1 = bf16[8,8,16,128]{3,2,1,0:T(8,128)(2,1)} custom-call(bf16[1024,128]{1,0:T(8,128)(2,1)S(1)} %copy-done.3), custom_call_target="tpu_custom_call" | custom-call | flops 1 | bytes 1 | tf_op jit(solution)/shard_map/filter_blocks/pallas_call | solution.py:196
  29.3 3.9 %all-to-all-start = ((bf16[8,8,16,128]{3,2,1,0:T(8,128)(2,1)}), bf16[8,8,16,128]{3,2,1,0:T(8,128)(2,1)S(1)}, u32[]{:S(2)}, u32[]{:S(2)}) async-start(bf16[8,8,16,128]{3,2,1,0:T(8,128)(2,1)} %filter_blocks.1), calls=%async_computation | async-start | bytes 524288 | tf_op jit(solution)/shard_map/all_to_all | solution.py:401
  33.2 0.5 collective-permute-start.4
  33.9 1.2 %collective-permute-done.4.came_a = bf16[1024,128]{1,0:T(8,128)(2,1)S(1)} collective-permute-done((bf16[1024,128]{1,0:T(8,128)(2,1)S(1)}, bf16[1024,128]{1,0:T(8,128)(2,1)S(1)}, u32[]{:S(2)}, u32[]{:S(2)}) %collective-permute-start.4) | collective-permute-done | bytes 262176 | tf_op jit(solution)/shard_map/ppermute | solution.py:358
  35.1 0.7 copy-done.4
  35.8 1.0 %copy-done.2 = f32[1024,128]{1,0:T(8,128)S(1)} copy-done((f32[1024,128]{1,0:T(8,128)S(1)}, f32[1024,128]{1,0:T(8,128)}, u32[]{:S(2)}) %copy-start.2) | copy-done | bytes 524312
  36.9 0.9 %copy-done.5 = bf16[1024,128]{1,0:T(8,128)(2,1)S(1)} copy-done((bf16[1024,128]{1,0:T(8,128)(2,1)S(1)}, bf16[1024,128]{1,0:T(8,128)(2,1)}, u32[]{:S(2)}) %copy-start.5) | copy-done | bytes 262168
  37.8 0.7 mix_rows.1
  38.5 0.7 copy-done.7
  39.3 4.9 %all-to-all-done = bf16[8,8,16,128]{3,2,1,0:T(8,128)(2,1)S(1)} async-done(((bf16[8,8,16,128]{3,2,1,0:T(8,128)(2,1)}), bf16[8,8,16,128]{3,2,1,0:T(8,128)(2,1)S(1)}, u32[]{:S(2)}, u32[]{:S(2)}) %all-to-all-start) | async-done | bytes 262176 | tf_op jit(solution)/shard_map/all_to_all | solution.py:401
  44.1 1.1 %gate.1 = bf16[4,16,16,128]{3,2,1,0:T(8,128)(2,1)} custom-call(f32[2064,128]{1,0:T(8,128)S(1)} %get-tuple-element.41.kept_ref, bf16[1,2064,128]{2,1,0:T(8,128)(2,1)S(1)} %bitcast.23, f32[3,128]{1,0:T(4,128)S(1)} %reshape.18.taps_ref), custom_call_target="tpu_custom_call" | custom-call | flops 1 | bytes 1 | tf_op jit(solution)/shard_map/gate/pallas_call | solution.py:232
  45.2 3.9 %all-to-all-start.1 = ((bf16[4,16,16,128]{3,2,1,0:T(8,128)(2,1)}), bf16[4,16,16,128]{3,2,1,0:T(8,128)(2,1)S(1)}, u32[]{:S(2)}, u32[]{:S(2)}) async-start(bf16[4,16,16,128]{3,2,1,0:T(8,128)(2,1)} %gate.1), calls=%async_computation.1 | async-start | bytes 524288 | tf_op jit(solution)/shard_map/all_to_all | solution.py:409
  49.1 1.5 %collective-permute-start.7 = (bf16[1040,128]{1,0:T(8,128)(2,1)}, bf16[1040,128]{1,0:T(8,128)(2,1)S(1)}, u32[]{:S(2)}, u32[]{:S(2)}) collective-permute-start(bf16[1040,128]{1,0:T(8,128)(2,1)} %bitcast.26), channel_id=1, source_target_pairs={{0,2},{2,0},{1,3},{3,1},{4,6},{6,4},{5,7},{7,5},{8,10},{10,8},{9,1... | collective-permute-start | bytes 798728 | tf_op jit(solution)/shard_map/ppermute | solution.py:358
  50.7 6.1 %collective-permute-done.7 = bf16[1040,128]{1,0:T(8,128)(2,1)S(1)} collective-permute-done((bf16[1040,128]{1,0:T(8,128)(2,1)}, bf16[1040,128]{1,0:T(8,128)(2,1)S(1)}, u32[]{:S(2)}, u32[]{:S(2)}) %collective-permute-start.7) | collective-permute-done | bytes 266272 | tf_op jit(solution)/shard_map/ppermute | solution.py:358
  56.8 0.7 all-to-all-done.1
  57.6 11.8 %long_conv.1 = bf16[1024,128]{1,0:T(8,128)(2,1)} custom-call(bf16[1024,128]{1,0:T(8,128)(2,1)S(1)} %bitcast.22, bf16[1024,128]{1,0:T(8,128)(2,1)S(1)} %bitcast.21, f32[1,16]{1,0:T(1,128)S(1)} %dynamic-slice_bitcast_fusion.3.bias_ref), custom_call_target="tpu_custom_call" | custom-call | flops 1 | bytes 1 | tf_op jit(solution)/shard_map/long_conv/pallas_call | solution.py:317
  69.3 4.9 %all-to-all-start.2 = ((bf16[8,8,16,128]{3,2,1,0:T(8,128)(2,1)}), bf16[8,8,16,128]{3,2,1,0:T(8,128)(2,1)S(1)}, u32[]{:S(2)}, u32[]{:S(2)}) async-start(bf16[8,8,16,128]{3,2,1,0:T(8,128)(2,1)} %bitcast.14), calls=%async_computation.2 | async-start | bytes 524288 | tf_op jit(solution)/shard_map/all_to_all | solution.py:414
  74.3 8.2 %all-to-all-done.2.z_ref = bf16[8,8,16,128]{3,2,1,0:T(8,128)(2,1)S(1)} async-done(((bf16[8,8,16,128]{3,2,1,0:T(8,128)(2,1)}), bf16[8,8,16,128]{3,2,1,0:T(8,128)(2,1)S(1)}, u32[]{:S(2)}, u32[]{:S(2)}) %all-to-all-start.2) | async-done | bytes 262176 | tf_op jit(solution)/shard_map/all_to_all | solution.py:414
  82.5 1.0 %finish.1 = bf16[1024,128]{1,0:T(8,128)(2,1)} custom-call(f32[1040,128]{1,0:T(8,128)S(1)} %get-tuple-element.40.kept_ref, bf16[1,1040,128]{2,1,0:T(8,128)(2,1)S(1)} %bitcast.24, f32[3,128]{1,0:T(4,128)S(1)} %bitcast.25, bf16[8,8,16,128]{3,2,1,0:T(8,128)(2,1)S(1)} %all-to-all-done.2.z_ref), custom_call_target="tpu_custom_call" | custom-call | flops 1 | bytes 1 | tf_op jit(solution)/shard_map/finish/pallas_call | solution.py:344
  (28 shorter events, 0.7 us)
Async XLA Ops:
  0.0 50.6 %copy-start = (f32[128]{0:T(128)S(1)}, f32[128]{0:T(128)}, u32[]{:S(2)}) copy-start(f32[128]{0:T(128)} %param.9) | copy-start | bytes 1540
  2.9 9.9 %collective-permute-start = (bf16[2048,384]{1,0:T(8,128)(2,1)}, bf16[2048,384]{1,0:T(8,128)(2,1)S(1)}, u32[]{:S(2)}, u32[]{:S(2)}) collective-permute-start(bf16[2048,384]{1,0:T(8,128)(2,1)} %pad_maximum_fusion), channel_id=1, source_target_pairs={{0,1},{1,0},{2,3},{3,2},{4,5},{5,4},{6,7},{7,6},{8,9},{9,8},{10,11... | collective-permute-start | bytes 4718600 | tf_op jit(solution)/shard_map/ppermute | solution.py:358
  4.2 13.7 %collective-permute-start.1 = (bf16[16,2048]{1,0:T(8,128)(2,1)S(1)}, bf16[16,2048]{1,0:T(8,128)(2,1)S(1)}, u32[]{:S(2)}, u32[]{:S(2)}) collective-permute-start(bf16[16,2048]{1,0:T(8,128)(2,1)S(1)} %slice.16), channel_id=1, source_target_pairs={{0,4},{4,8},{8,12},{1,5},{5,9},{9,13},{2,6},{6,10},{10,14},{3,7},{... | collective-permute-start | bytes 196616 | tf_op jit(solution)/shard_map/ppermute | solution.py:387
  17.1 0.8 copy-start.1
  22.6 4.4 %copy-start.6 = (bf16[1040,128]{1,0:T(8,128)(2,1)}, bf16[1040,128]{1,0:T(8,128)(2,1)S(1)}, u32[]{:S(2)}) copy-start(bf16[1040,128]{1,0:T(8,128)(2,1)S(1)} %get-tuple-element.39) | copy-start | bytes 798724
  22.6 5.9 %copy-start.3 = (bf16[1024,128]{1,0:T(8,128)(2,1)S(1)}, bf16[1024,128]{1,0:T(8,128)(2,1)}, u32[]{:S(2)}) copy-start(bf16[1024,128]{1,0:T(8,128)(2,1)} %h_ref) | copy-start | bytes 786436
  22.6 11.1 %copy-start.8 = (f32[3,3,128]{2,1,0:T(4,128)S(1)}, f32[3,3,128]{2,1,0:T(4,128)}, u32[]{:S(2)}) copy-start(f32[3,3,128]{2,1,0:T(4,128)} %param.7) | copy-start | bytes 13828
  22.6 2.7 %collective-permute-start.3 = (bf16[2,1040,128]{2,1,0:T(8,128)(2,1)S(1)}, bf16[2,1040,128]{2,1,0:T(8,128)(2,1)S(1)}, u32[]{:S(2)}, u32[]{:S(2)}) collective-permute-start(bf16[2,1040,128]{2,1,0:T(8,128)(2,1)S(1)} %get-tuple-element.35), channel_id=1, source_target_pairs={{0,1},{1,0},{2,3},{3,2},{4,5},{5,4},{6,7},{7,6},{8,9},{9,8},{10,11... | collective-permute-start | bytes 1597448 | tf_op jit(solution)/shard_map/ppermute | solution.py:358
  22.9 2.4 %collective-permute-start.2 = (bf16[2,1024,128]{2,1,0:T(8,128)(2,1)S(1)}, bf16[2,1024,128]{2,1,0:T(8,128)(2,1)S(1)}, u32[]{:S(2)}, u32[]{:S(2)}) collective-permute-start(bf16[2,1024,128]{2,1,0:T(8,128)(2,1)S(1)} %get-tuple-element.33), channel_id=1, source_target_pairs={{0,1},{1,0},{2,3},{3,2},{4,5},{5,4},{6,7},{7,6},{8,9},{9,8},{10,11... | collective-permute-start | bytes 1572872 | tf_op jit(solution)/shard_map/ppermute | solution.py:358
  27.0 17.2 %collective-permute-start.6 = (bf16[2064,128]{1,0:T(8,128)(2,1)}, bf16[2064,128]{1,0:T(8,128)(2,1)S(1)}, u32[]{:S(2)}, u32[]{:S(2)}) collective-permute-start(bf16[2064,128]{1,0:T(8,128)(2,1)} %bitcast.6), channel_id=1, source_target_pairs={{0,2},{2,0},{1,3},{3,1},{4,6},{6,4},{5,7},{7,5},{8,10},{10,8},{9,1... | collective-permute-start | bytes 1585160 | tf_op jit(solution)/shard_map/ppermute | solution.py:358
  28.5 45.8 %slice-start = ((f32[3,3,128]{2,1,0:T(4,128)}), f32[3,1,128]{2,1,0:T(1,128)S(1)}, s32[]{:S(2)}) async-start(f32[3,3,128]{2,1,0:T(4,128)} %param.7), calls=%async_computation.3 | async-start | bytes 3072 | tf_op jit(solution)/shard_map/slice | solution.py:415
  29.3 14.8 %all-to-all-start = ((bf16[8,8,16,128]{3,2,1,0:T(8,128)(2,1)}), bf16[8,8,16,128]{3,2,1,0:T(8,128)(2,1)S(1)}, u32[]{:S(2)}, u32[]{:S(2)}) async-start(bf16[8,8,16,128]{3,2,1,0:T(8,128)(2,1)} %filter_blocks.1), calls=%async_computation | async-start | bytes 524288 | tf_op jit(solution)/shard_map/all_to_all | solution.py:401
  33.2 2.6 %collective-permute-start.5 = (bf16[1040,128]{1,0:T(8,128)(2,1)}, bf16[1040,128]{1,0:T(8,128)(2,1)S(1)}, u32[]{:S(2)}, u32[]{:S(2)}) collective-permute-start(bf16[1040,128]{1,0:T(8,128)(2,1)} %copy-done.6), channel_id=1, source_target_pairs={{0,1},{1,0},{2,3},{3,2},{4,5},{5,4},{6,7},{7,6},{8,9},{9,8},{10,11... | collective-permute-start | bytes 798728 | tf_op jit(solution)/shard_map/ppermute | solution.py:358
  33.2 1.9 %collective-permute-start.4 = (bf16[1024,128]{1,0:T(8,128)(2,1)S(1)}, bf16[1024,128]{1,0:T(8,128)(2,1)S(1)}, u32[]{:S(2)}, u32[]{:S(2)}) collective-permute-start(bf16[1024,128]{1,0:T(8,128)(2,1)S(1)} %get-tuple-element.37), channel_id=1, source_target_pairs={{0,1},{1,0},{2,3},{3,2},{4,5},{5,4},{6,7},{7,6},{8,9},{9,8},{10,11... | collective-permute-start | bytes 786440 | tf_op jit(solution)/shard_map/ppermute | solution.py:358
  35.1 0.7 copy-start.4
  35.8 1.0 %copy-start.2 = (f32[1024,128]{1,0:T(8,128)S(1)}, f32[1024,128]{1,0:T(8,128)}, u32[]{:S(2)}) copy-start(f32[1024,128]{1,0:T(8,128)} %copy-done.1) | copy-start | bytes 1572868
  36.8 0.9 %copy-start.5 = (bf16[1024,128]{1,0:T(8,128)(2,1)S(1)}, bf16[1024,128]{1,0:T(8,128)(2,1)}, u32[]{:S(2)}) copy-start(bf16[1024,128]{1,0:T(8,128)(2,1)} %copy-done.4) | copy-start | bytes 786436
  38.5 0.7 copy-start.7
  45.2 12.3 %all-to-all-start.1 = ((bf16[4,16,16,128]{3,2,1,0:T(8,128)(2,1)}), bf16[4,16,16,128]{3,2,1,0:T(8,128)(2,1)S(1)}, u32[]{:S(2)}, u32[]{:S(2)}) async-start(bf16[4,16,16,128]{3,2,1,0:T(8,128)(2,1)} %gate.1), calls=%async_computation.1 | async-start | bytes 524288 | tf_op jit(solution)/shard_map/all_to_all | solution.py:409
  49.1 7.7 %collective-permute-start.7 = (bf16[1040,128]{1,0:T(8,128)(2,1)}, bf16[1040,128]{1,0:T(8,128)(2,1)S(1)}, u32[]{:S(2)}, u32[]{:S(2)}) collective-permute-start(bf16[1040,128]{1,0:T(8,128)(2,1)} %bitcast.26), channel_id=1, source_target_pairs={{0,2},{2,0},{1,3},{3,1},{4,6},{6,4},{5,7},{7,5},{8,10},{10,8},{9,1... | collective-permute-start | bytes 798728 | tf_op jit(solution)/shard_map/ppermute | solution.py:358
  69.3 13.1 %all-to-all-start.2 = ((bf16[8,8,16,128]{3,2,1,0:T(8,128)(2,1)}), bf16[8,8,16,128]{3,2,1,0:T(8,128)(2,1)S(1)}, u32[]{:S(2)}, u32[]{:S(2)}) async-start(bf16[8,8,16,128]{3,2,1,0:T(8,128)(2,1)} %bitcast.14), calls=%async_computation.2 | async-start | bytes 524288 | tf_op jit(solution)/shard_map/all_to_all | solution.py:414
